TPU v7x, 256 devices: a whole 4x4x8 slice. The times are simulated.
256 devices in a mesh: seq: 32 (over y, x, core), tp: 8 (over z).
Axes of the slice: x: 4, y: 4, z: 8, core: 2. Of those that a mesh axis runs over, the one named last changes fastest.
Arguments:
- queries: bfloat16 [32, 64, 4096], P('seq', None, 'tp'), may hold values from -8 to 8
- draft_kv: bfloat16 [32, 64, 8, 128], P('seq', None, 'tp'), may hold values from -12.5 to 12.5
- cache_kv: bfloat16 [8, 16384, 8, 128], P(None, 'seq', 'tp'), may hold values from -10 to 10
- cache_len: int32 [8], replicated, may hold values from 4096 to 16384
- group_of: int32 [32], replicated, may hold values from 0 to 7, as said below
- parents: int32 [32, 64], P('seq'), may hold values from 0 to 62, as said below
- sink_logit: float32 [64], P('tp'), may hold values from 4 to 20
- w_out: bfloat16 [4096, 2880], P('tp'), may hold values from -0.09375 to 0.09375
- hidden_in: bfloat16 [2048, 2880], P('seq', 'tp'), may hold values from -3 to 3
- norm_gain: float32 [2880], replicated, may hold values from 0.5 to 1.5
- routes: int32 [2048, 4], P('seq'), may hold values from 0 to 31, all different within a row; in each aligned block of 64 rows (0 to 63, 64 to 127, ...) at most 16 rows name the same one
- route_weight: float32 [2048, 4], P('seq'), may hold values from 0.1 to 1
- w_gate_up: bfloat16 [32, 2, 2880, 2880], P('seq', None, None, 'tp'), may hold values from -0.109375 to 0.109375
- w_down: bfloat16 [32, 2880, 2880], P('seq', 'tp'), may hold values from -0.109375 to 0.109375
- accepted_idx: int32 [32, 16], P('seq'), may hold values from 0 to 45, as said below
- accepted_len: int32 [32], P('seq'), may hold values from 1 to 16, as said below
- tail_slot: int32 [32], replicated, may hold values from 0 to 31, each once
Outputs:
- out_hidden: bfloat16 [2048, 2880], P('seq', 'tp')
- new_tail: bfloat16 [32, 16, 8, 128], P('seq', None, 'tp')
Inputs may be any that keep to these rules, and one draw needn't show every extreme that they name: `parents`: node 0 of every tree is its root and its own parent; every other node's parent is one of the three nodes before it. `accepted_idx`: row r lists the first 16 nodes of a path from the root of request r's tree down to one of its last four nodes, root first. `accepted_len`: each request accepts one or more nodes. `group_of`: every prompt group has exactly 4 requests. `routes`: the 4 experts of a token differ; at most 16 of one device's rows (one aligned block of 64 tokens) name one expert.
All inputs are finite; a program needn't handle non-finite values.
Results may differ from a plain program's by a relative error of at most 0.025.
Values may be sent and summed in bfloat16 or wider, within the bound.
A program may use at most 128 MiB of HBM per device.

v0:
```python
import jax
import jax.numpy as jnp
from jax import lax
from jax.sharding import PartitionSpec as P

HQ = 64
KVH = 8
HD = 64


def ancestry(parents):
    tree_len = parents.shape[1]
    node_ids = jnp.arange(tree_len, dtype=jnp.int32)
    linked = (parents[:, :, None] == node_ids[None, None, :]) | (
        node_ids[:, None] == node_ids[None, :]
    )[None]
    reachable = linked.astype(jnp.float32)
    for repeat in range((tree_len - 1).bit_length()):
        reachable = jnp.minimum(
            jnp.einsum("rij,rjk->rik", reachable, reachable, precision=lax.Precision.HIGHEST), 1.0
        )
    return reachable


def cache_block(block_queries, block_groups, cache_kv, cache_len, positions):
    block_rows, tree_len, head_cols = block_queries.shape
    kv_dev = cache_kv.shape[2]
    grouped = block_queries.reshape(block_rows, tree_len, kv_dev, HQ // KVH, HD)
    picked = jnp.take(cache_kv, block_groups, axis=0)
    cache_keys = picked[..., :HD]
    cache_values = picked[..., HD:]
    scores = (
        jnp.einsum("rtkqd,rckd->rkqtc", grouped, cache_keys, preferred_element_type=jnp.float32)
        * 0.125
    )
    lengths = jnp.take(cache_len, block_groups)
    usable = (positions[None, :] < lengths[:, None])[:, None, None, None, :]
    masked = jnp.where(usable, scores, -1e30)
    shard_max = jnp.max(masked, axis=-1)
    weights = jnp.where(usable, jnp.exp(masked - shard_max[..., None]), 0.0)
    shard_sum = jnp.sum(weights, axis=-1)
    shard_out = jnp.einsum(
        "rkqtc,rckd->rkqtd",
        weights.astype(jnp.bfloat16),
        cache_values,
        preferred_element_type=jnp.float32,
    )
    shard_out = (shard_out / jnp.maximum(shard_sum, 1.0)[..., None]).astype(jnp.bfloat16)
    out_rows = shard_out.transpose(0, 3, 1, 2, 4).reshape(block_rows, tree_len, head_cols)
    max_rows = shard_max.transpose(0, 3, 1, 2).reshape(block_rows, tree_len, -1)
    sum_rows = shard_sum.transpose(0, 3, 1, 2).reshape(block_rows, tree_len, -1)
    return (out_rows, max_rows, sum_rows)


def expert_rows(arrived, w_gate_up, w_down):
    exp_dev = w_gate_up.shape[0]
    sources = arrived.shape[0] // exp_dev
    grouped = arrived.reshape(sources, exp_dev, arrived.shape[1], arrived.shape[2])
    gate_proj = jnp.einsum(
        "sexd,edf->sexf", grouped, w_gate_up[:, 0], preferred_element_type=jnp.float32
    )
    upward = jnp.einsum(
        "sexd,edf->sexf", grouped, w_gate_up[:, 1], preferred_element_type=jnp.float32
    )
    active = (gate_proj * jax.nn.sigmoid(1.702 * gate_proj) * (upward + 1.0)).astype(jnp.bfloat16)
    down_part = jnp.einsum("sexf,efd->sexd", active, w_down, preferred_element_type=jnp.float32)
    return down_part.reshape(arrived.shape[0], arrived.shape[1], -1)


def shards(
    queries,
    draft_kv,
    cache_kv,
    cache_len,
    group_of,
    parents,
    sink_logit,
    w_out,
    hidden_in,
    norm_gain,
    routes,
    route_weight,
    w_gate_up,
    w_down,
    accepted_idx,
    accepted_len,
    tail_slot,
):
    seq_count = lax.axis_size("seq")
    req_dev, tree_len, head_cols = queries.shape
    kv_dev = cache_kv.shape[2]
    per_kv = HQ // KVH
    heads_dev = kv_dev * per_kv
    shard_len = cache_kv.shape[1]
    positions = lax.axis_index("seq") * shard_len + jnp.arange(shard_len, dtype=jnp.int32)
    every_query = lax.all_gather(queries, "seq", axis=0, tiled=True)
    requests_all = every_query.shape[0]
    block_count = requests_all // 8
    stacked = (
        every_query.reshape(block_count, 8, tree_len, head_cols),
        group_of.reshape(block_count, 8),
    )
    shard_out, shard_max, shard_sum = lax.map(
        lambda blocks: cache_block(blocks[0], blocks[1], cache_kv, cache_len, positions), stacked
    )
    shard_out = shard_out.reshape(seq_count, req_dev, tree_len, head_cols)
    shard_max = shard_max.reshape(seq_count, req_dev, tree_len, heads_dev)
    shard_sum = shard_sum.reshape(seq_count, req_dev, tree_len, heads_dev)
    came_out = lax.all_to_all(shard_out, "seq", split_axis=0, concat_axis=0, tiled=True)
    came_max, came_sum = (
        lax.all_to_all(shard_max, "seq", split_axis=0, concat_axis=0, tiled=True),
        lax.all_to_all(shard_sum, "seq", split_axis=0, concat_axis=0, tiled=True),
    )
    reachable = ancestry(parents)
    own_heads = queries.reshape(req_dev, tree_len, kv_dev, per_kv, HD)
    draft_keys = draft_kv[..., :HD]
    draft_values = draft_kv[..., HD:]
    tree_scores = (
        jnp.einsum("rtkqd,rukd->rkqtu", own_heads, draft_keys, preferred_element_type=jnp.float32)
        * 0.125
    )
    allowed = (reachable > 0.5)[:, None, None, :, :]
    tree_masked = jnp.where(allowed, tree_scores, -1e30)
    tree_max = jnp.max(tree_masked, axis=-1)
    tree_weight = jnp.where(allowed, jnp.exp(tree_masked - tree_max[..., None]), 0.0)
    tree_sum = jnp.sum(tree_weight, axis=-1)
    tree_num = jnp.einsum(
        "rkqtu,rukd->rkqtd",
        tree_weight.astype(jnp.bfloat16),
        draft_values,
        preferred_element_type=jnp.float32,
    )
    tree_max = tree_max.transpose(0, 3, 1, 2).reshape(req_dev, tree_len, heads_dev)
    tree_sum = tree_sum.transpose(0, 3, 1, 2).reshape(req_dev, tree_len, heads_dev)
    tree_num = tree_num.transpose(0, 3, 1, 2, 4).reshape(req_dev, tree_len, heads_dev, HD)
    sink_rows = sink_logit[None, None, :]
    ceiling = jnp.maximum(jnp.maximum(jnp.max(came_max, axis=0), tree_max), sink_rows)
    shard_scale = came_sum * jnp.exp(came_max - ceiling[None])
    tree_scale = jnp.exp(tree_max - ceiling)
    denominator = (
        jnp.sum(shard_scale, axis=0) + tree_scale * tree_sum + jnp.exp(sink_rows - ceiling)
    )
    weighted = jnp.sum(
        shard_scale[..., None]
        * came_out.reshape(seq_count, req_dev, tree_len, heads_dev, HD).astype(jnp.float32),
        axis=0,
    )
    numerator = weighted + tree_scale[..., None] * tree_num
    attention = (
        (numerator / denominator[..., None])
        .reshape(req_dev * tree_len, heads_dev * HD)
        .astype(jnp.bfloat16)
    )
    projected = jnp.dot(attention, w_out, preferred_element_type=jnp.float32)
    width_dev = hidden_in.shape[1]
    tp_index = lax.axis_index("tp")
    summed = lax.psum(projected, "tp")
    resid_full = lax.all_gather(hidden_in, "tp", axis=1, tiled=True)
    stream = (resid_full.astype(jnp.float32) + summed).astype(jnp.bfloat16)
    stream_f = stream.astype(jnp.float32)
    inv_scale = lax.rsqrt(jnp.mean(stream_f * stream_f, axis=-1, keepdims=True) + 1e-05)
    normed_full = (stream_f * inv_scale * norm_gain[None, :]).astype(jnp.bfloat16)
    stream_cols = lax.dynamic_slice_in_dim(stream, tp_index * width_dev, width_dev, 1)
    tok_dev = routes.shape[0]
    top_count = routes.shape[1]
    exp_dev = w_gate_up.shape[0]
    experts_all = seq_count * exp_dev
    capacity = 2 * tok_dev * top_count // experts_all
    flat_routes = routes.reshape(-1)
    onehot = (flat_routes[:, None] == jnp.arange(experts_all, dtype=jnp.int32)[None, :]).astype(
        jnp.int32
    )
    position = jnp.sum((jnp.cumsum(onehot, axis=0) - onehot) * onehot, axis=1)
    slot_ids = flat_routes * capacity + position
    buckets = jnp.arange(experts_all * capacity, dtype=jnp.int32)
    placing = jnp.sum(
        (slot_ids.reshape(tok_dev, top_count)[None, :, :] == buckets[:, None, None]).astype(
            jnp.int32
        ),
        axis=2,
    ).astype(jnp.bfloat16)
    dispatched = (
        jnp.dot(placing, normed_full, preferred_element_type=jnp.float32)
        .astype(jnp.bfloat16)
        .reshape(experts_all, capacity, -1)
    )
    down_part = expert_rows(
        lax.all_to_all(dispatched, "seq", split_axis=0, concat_axis=0, tiled=True),
        w_gate_up,
        w_down,
    )
    expert_out = lax.psum_scatter(
        down_part.astype(jnp.bfloat16), "tp", scatter_dimension=2, tiled=True
    )
    returned = lax.all_to_all(expert_out, "seq", split_axis=0, concat_axis=0, tiled=True)
    gathered_rows = jnp.take(
        returned.reshape(experts_all * capacity, -1), slot_ids, axis=0
    ).reshape(tok_dev, top_count, -1)
    mixture = jnp.sum(route_weight[:, :, None] * gathered_rows.astype(jnp.float32), axis=1)
    out_hidden = (stream_cols.astype(jnp.float32) + mixture).astype(jnp.bfloat16)
    blk_len = accepted_idx.shape[1]
    chosen = draft_kv[jnp.arange(req_dev, dtype=jnp.int32)[:, None], accepted_idx]
    kept_rows = jnp.arange(blk_len, dtype=jnp.int32)[None, :] < accepted_len[:, None]
    picked_rows = jnp.where(kept_rows[:, :, None, None], chosen, jnp.zeros_like(chosen))
    everyone = lax.all_gather(picked_rows, "seq", axis=0, tiled=True)
    my_slots = lax.axis_index("seq") * req_dev + jnp.arange(req_dev, dtype=jnp.int32)
    selector = (tail_slot[None, :] == my_slots[:, None]).astype(jnp.bfloat16)
    new_tail = jnp.dot(
        selector, everyone.reshape(everyone.shape[0], -1), preferred_element_type=jnp.float32
    ).astype(jnp.bfloat16)
    new_tail = new_tail.reshape(req_dev, blk_len, kv_dev, -1)
    return (out_hidden, new_tail)


def solution(mesh):
    in_specs = (
        P("seq", None, "tp"),
        P("seq", None, "tp", None),
        P(None, "seq", "tp", None),
        P(),
        P(),
        P("seq", None),
        P("tp"),
        P("tp", None),
        P("seq", "tp"),
        P(),
        P("seq", None),
        P("seq", None),
        P("seq", None, None, "tp"),
        P("seq", "tp", None),
        P("seq", None),
        P("seq"),
        P(),
    )
    out_specs = (P("seq", "tp"), P("seq", None, "tp", None))
    return jax.shard_map(shards, mesh=mesh, in_specs=in_specs, out_specs=out_specs, check_vma=False)
```

profile of v0, /device:TPU:1, one launch (start us, length us, event | category | flops | bytes accessed | tf_op | source)
XLA Modules:
  0.0 533.3 jit_solution(3878875501359007208)
XLA Ops:
  8.8 1.5 convolution_minimum_fusion.5
  10.3 53.3 %all-gather.3.cloned.1.call-done = bf16[32,64,512]{2,1,0:T(8,128)(2,1)} async-done(((bf16[1,64,512]{2,1,0:T(8,128)(2,1)}), bf16[32,64,512]{2,1,0:T(8,128)(2,1)}) %all-gather.3.cloned.1.call-update) | async-done | bytes 2097168 | tf_op jit(solution)/shard_map/all_gather | solution.py:96
  63.7 97.3 %while.15 = (s32[]{:T(128)}, bf16[4,8,64,512]{3,2,1,0:T(8,128)(2,1)}, f32[4,8,64,8]{2,3,1,0:T(8,128)}, f32[4,8,64,8]{2,3,1,0:T(8,128)}, s32[4,8]{1,0:T(4,128)S(1...) while((s32[]{:T(128)}, ...), condition=%wide.region_3.4_spmd.clone, body=%wide.region_0.3_spmd.clone.sunk | while | flops 565184128 | bytes 43791872 | solution.py:103
  65.0 2.9 gather_fusion.1
  67.9 2.3 copy.129
  70.2 2.4 bitcast_select_fusion.4
  75.3 2.7 bitcast_reduce_fusion.3
  78.0 2.3 fusion.128
  80.9 2.6 fusion.129
  83.6 1.7 copy.130
  85.3 1.9 broadcast_in_dim.201
  89.4 2.9 gather_fusion.1
  92.3 2.3 copy.129
  94.5 2.4 bitcast_select_fusion.4
  99.6 2.7 bitcast_reduce_fusion.3
  102.3 2.3 fusion.128
  105.3 2.6 fusion.129
  107.9 1.7 copy.130
  109.6 1.9 broadcast_in_dim.201
  113.7 2.9 gather_fusion.1
  116.6 2.3 copy.129
  118.9 2.4 bitcast_select_fusion.4
  124.0 2.7 bitcast_reduce_fusion.3
  126.7 2.3 fusion.128
  129.6 2.6 fusion.129
  132.2 1.7 copy.130
  133.9 1.9 broadcast_in_dim.201
  138.0 2.9 gather_fusion.1
  140.9 2.3 copy.129
  143.2 2.4 bitcast_select_fusion.4
  148.3 2.7 bitcast_reduce_fusion.3
  151.0 2.3 fusion.128
  153.9 2.6 fusion.129
  156.5 1.7 copy.130
  158.2 1.9 broadcast_in_dim.201
  161.0 1.7 reshape.754
  162.7 5.1 all-to-all-start.1
  168.8 1.7 reshape.752
  170.4 4.7 all-to-all-done.1
  175.1 3.9 all-to-all-start
  180.8 5.6 %all-to-all-done = f32[32,1,512]{2,1,0:T(1,128)S(1)} async-done(((f32[32,1,512]{2,1,0:T(1,128)}), f32[32,1,512]{2,1,0:T(1,128)S(1)}, u32[]{:S(2)}, u32[]{:S(2)}) %all-to-all-start) | async-done | bytes 65568 | tf_op jit(solution)/shard_map/all_to_all | solution.py:112
  186.4 4.7 all-to-all-start.2
  193.3 23.3 %all-gather = bf16[8,360,64]{1,2,0:T(8,128)(2,1)S(1)} all-gather(bf16[1,360,64]{1,2,0:T(8,128)(2,1)} %bitcast.318), channel_id=1, replica_groups=mesh['seq'=32,'tp'=8] {'tp'}, dimensions={0}, use_global_device_ids=true | all-gather | bytes 414720 | tf_op jit(solution)/shard_map/all_gather | solution.py:158
  217.7 2.3 reshape.728
  227.4 5.9 %mul.135 = f32[32,64,8,64]{3,2,1,0:T(8,128)} broadcast(f32[32,64,8]{2,1,0:T(8,128)} %copy.92), dimensions={0,1,2} | broadcast | bytes 4259840 | tf_op jit(solution)/shard_map/mul | solution.py:144
  233.4 7.5 %mul.136 = f32[32,1,64,512]{3,2,1,0:T(8,128)} reshape(f32[32,64,8,64]{3,2,1,0:T(8,128)} %mul.135) | data formatting | bytes 8388608 | tf_op jit(solution)/shard_map/mul | solution.py:144
  240.9 3.6 multiply_reduce_fusion
  244.5 1.9 fusion.77
  247.8 72.6 %all-reduce.3.cloned.1.call-done = f32[64,2880]{1,0:T(8,128)} async-done(((f32[64,2880]{1,0:T(8,128)}), f32[64,2880]{1,0:T(8,128)}) %all-reduce.3.cloned.1.call-update) | async-done | bytes 737296 | tf_op jit(solution)/shard_map/psum | solution.py:157
  322.7 2.7 convolution_convert_fusion.1
  325.4 4.6 copy.103
  329.9 50.3 %all_to_all.25 = bf16[32,16,2880]{2,1,0:T(8,128)(2,1)S(1)} all-to-all(bf16[32,16,2880]{2,1,0:T(8,128)(2,1)} %bitcast.309), channel_id=1, replica_groups=mesh['seq'=32,'tp'=8] {'seq'}, dimensions={0} | all-to-all | bytes 5898240 | tf_op jit(solution)/shard_map/all_to_all | solution.py:188
  380.2 1.6 copy-done.2
  381.9 4.2 fusion.27
  386.1 8.5 %convolution_convert_fusion = bf16[32,16,2880]{2,1,0:T(8,128)(2,1)} fusion(bf16[1,360,2880]{2,1,0:T(8,128)(2,1)} %param.32, bf16[32,16,2880]{2,1,0:T(8,128)(2,1)} %copy-done.2, bf16[1,2,2880,360]{2,3,1,0:T(8,128)(2,1)} %param.31, f32[32,1,16,360]{3,2,0,1:T(8,128)} %fusion.27), kind=kOutput, calls=%fused_computation.40 | convolution fusion | flops 2126315520 | bytes 10989568 | tf_op jit(solution)/shard_map/sexf,efd->sexd/dot_general | solution.py:66
  394.6 21.4 %copy.108 = bf16[32,16,2880]{1,0,2:T(8,128)(2,1)} copy(bf16[32,16,2880]{2,1,0:T(8,128)(2,1)} %convolution_convert_fusion) | data formatting | bytes 5898240
  416.0 39.5 %reshape.749 = bf16[2880,512]{1,0:T(8,128)(2,1)} reshape(bf16[2880,32,16]{2,1,0:T(8,128)(2,1)} %bitcast.306) | data formatting | bytes 5898240
  457.1 22.6 %all_gather.11 = bf16[32,16,1,128]{3,1,2,0:T(8,128)(2,1)S(1)} all-gather(bf16[1,16,1,128]{3,1,2,0:T(8,128)(2,1)S(1)} %bitcast_select_fusion.2), channel_id=1, replica_groups=mesh['seq'=32,'tp'=8] {'seq'}, dimensions={0}, use_global_device_ids=true | all-gather | bytes 135168 | tf_op jit(solution)/shard_map/all_gather | solution.py:205
  479.9 12.3 %reduce-scatter.4.cloned.1.call-done = bf16[360,512]{1,0:T(8,128)(2,1)} async-done(((bf16[2880,512]{1,0:T(8,128)(2,1)}), bf16[360,512]{1,0:T(8,128)(2,1)}) %reduce-scatter.4.cloned.1.call-update) | async-done | bytes 368656
  492.2 4.4 reshape.750
  496.5 5.0 copy.109
  501.6 11.1 %all-to-all-start.4 = ((bf16[32,16,360]{2,1,0:T(8,128)(2,1)}), bf16[32,16,360]{2,1,0:T(8,128)(2,1)S(1)}, u32[]{:S(2)}, u32[]{:S(2)}) async-start(bf16[32,16,360]{2,1,0:T(8,128)(2,1)} %copy.109), calls=%async_computation.4 | async-start | bytes 786432 | tf_op jit(solution)/shard_map/all_to_all | solution.py:195
  514.1 8.7 %all-to-all-done.4 = bf16[32,16,360]{2,1,0:T(8,128)(2,1)S(1)} async-done(((bf16[32,16,360]{2,1,0:T(8,128)(2,1)}), bf16[32,16,360]{2,1,0:T(8,128)(2,1)S(1)}, u32[]{:S(2)}, u32[]{:S(2)}) %all-to-all-start.4) | async-done | bytes 368672 | tf_op jit(solution)/shard_map/all_to_all | solution.py:195
  525.2 1.6 add_convert_fusion
  (162 shorter events, 45.4 us)
Async XLA Ops:
  7.2 237.3 %copy-start = (bf16[512,2880]{0,1:T(8,128)(2,1)S(1)}, bf16[512,2880]{0,1:T(8,128)(2,1)}, u32[]{:S(2)}) copy-start(bf16[512,2880]{0,1:T(8,128)(2,1)} %param.26) | copy-start | bytes 8847364
  7.2 56.5 %all-gather.3.cloned.1.call-start = ((), (), s32[]{:S(2)}) async-start(), calls=%async_computation.6 | async-start | bytes 2162688 | tf_op jit(solution)/shard_map/all_gather | solution.py:96
  63.7 115.5 %copy-start.6 = (bf16[1,64,512]{2,1,0:T(8,128)(2,1)S(1)}, bf16[1,64,512]{2,1,0:T(8,128)(2,1)}, u32[]{:S(2)}) copy-start(bf16[1,64,512]{2,1,0:T(8,128)(2,1)} %param.19) | copy-start | bytes 196612
  63.7 115.6 %copy-start.13 = (s32[64,4]{0,1:T(4,128)S(1)}, s32[64,4]{0,1:T(4,128)}, u32[]{:S(2)}) copy-start(s32[64,4]{0,1:T(4,128)} %param.29) | copy-start | bytes 3076
  78.0 3.0 copy-start.1
  102.3 3.0 copy-start.1
  126.6 3.0 copy-start.1
  150.9 3.0 copy-start.1
  161.0 30.9 %copy-start.7 = (bf16[1,64,1,128]{3,1,2,0:T(8,128)(2,1)S(1)}, bf16[1,64,1,128]{3,1,2,0:T(8,128)(2,1)}, u32[]{:S(2)}) copy-start(bf16[1,64,1,128]{3,1,2,0:T(8,128)(2,1)} %param.20) | copy-start | bytes 49156
  162.7 12.4 %all-to-all-start.1 = ((f32[32,1,512]{2,1,0:T(1,128)}), f32[32,1,512]{2,1,0:T(1,128)S(1)}, u32[]{:S(2)}, u32[]{:S(2)}) async-start(f32[32,1,512]{2,1,0:T(1,128)} %reshape.754), calls=%async_computation.1 | async-start | bytes 131072 | tf_op jit(solution)/shard_map/all_to_all | solution.py:111
  175.1 17.0 %copy-start.9 = (f32[32,1,512]{2,1,0:T(1,128)}, f32[32,1,512]{2,1,0:T(1,128)S(1)}, u32[]{:S(2)}) copy-start(f32[32,1,512]{2,1,0:T(1,128)S(1)} %all-to-all-done.1) | copy-start | bytes 196612
  175.1 11.3 %all-to-all-start = ((f32[32,1,512]{2,1,0:T(1,128)}), f32[32,1,512]{2,1,0:T(1,128)S(1)}, u32[]{:S(2)}, u32[]{:S(2)}) async-start(f32[32,1,512]{2,1,0:T(1,128)} %reshape.752), calls=%async_computation | async-start | bytes 131072 | tf_op jit(solution)/shard_map/all_to_all | solution.py:112
  186.4 4.8 copy-start.11
  186.4 54.4 %all-to-all-start.2 = ((bf16[32,1,64,512]{3,2,1,0:T(8,128)(2,1)}), bf16[32,1,64,512]{3,2,1,0:T(8,128)(2,1)}, u32[]{:S(2)}, u32[]{:S(2)}) async-start(bf16[32,1,64,512]{3,2,1,0:T(8,128)(2,1)} %bitcast.313), calls=%async_computation.2 | async-start | bytes 4194304 | tf_op jit(solution)/shard_map/all_to_all | solution.py:109
  191.2 129.2 %all-reduce.3.cloned.1.call-start = ((), (), s32[]{:S(2)}) async-start(), calls=%async_computation.7 | async-start | bytes 1507328 | tf_op jit(solution)/shard_map/psum | solution.py:157
  192.4 28.8 %copy-start.10 = (f32[32,1,512]{2,1,0:T(1,128)S(1)}, f32[32,1,512]{2,1,0:T(1,128)}, u32[]{:S(2)}) copy-start(f32[32,1,512]{2,1,0:T(1,128)} %copy-done.9) | copy-start | bytes 196612
  193.3 28.8 %copy-start.12 = (f32[32,1,512]{2,1,0:T(1,128)S(1)}, f32[32,1,512]{2,1,0:T(1,128)}, u32[]{:S(2)}) copy-start(f32[32,1,512]{2,1,0:T(1,128)} %copy-done.11) | copy-start | bytes 196612
  240.9 3.6 copy-start.4
  240.9 3.6 copy-start.5
  244.5 2.0 copy-start.16
  244.5 2.8 copy-start.15
  244.5 78.2 %copy-start.14 = (f32[2880]{0:T(1024)S(1)}, f32[2880]{0:T(1024)}, u32[]{:S(2)}) copy-start(f32[2880]{0:T(1024)} %param.28) | copy-start | bytes 34564
  246.4 245.7 %reduce-scatter.4.cloned.1.call-start = ((), (), s32[]{:S(2)}) async-start(), calls=%async_computation.8 | async-start | bytes 3317760
  321.9 0.8 copy-start.3
  380.2 1.6 copy-start.2
  455.4 0.9 copy-start.19
  455.4 1.0 copy-start.8
  455.4 24.3 %copy-start.18 = (s32[32]{0:T(128)S(1)}, s32[32]{0:T(128)}, u32[]{:S(2)}) copy-start(s32[32]{0:T(128)} %param.35) | copy-start | bytes 388
  479.8 33.0 %copy-start.17 = (f32[64,4]{0,1:T(4,128)S(1)}, f32[64,4]{0,1:T(4,128)}, u32[]{:S(2)}) copy-start(f32[64,4]{0,1:T(4,128)} %param.30) | copy-start | bytes 3076
  501.6 21.3 %all-to-all-start.4 = ((bf16[32,16,360]{2,1,0:T(8,128)(2,1)}), bf16[32,16,360]{2,1,0:T(8,128)(2,1)S(1)}, u32[]{:S(2)}, u32[]{:S(2)}) async-start(bf16[32,16,360]{2,1,0:T(8,128)(2,1)} %copy.109), calls=%async_computation.4 | async-start | bytes 786432 | tf_op jit(solution)/shard_map/all_to_all | solution.py:195
Sparse Core Ops, SparseCore 0:
  10.6 53.0 all-gather.2
  246.5 73.8 all-reduce.2
  455.6 36.5 reduce-scatter.3
where the time goes:
time: 536 us; the launch traced here: 533 us
  local copies, waits for them, and re-layouts  164 us (31%)
  waiting for transfers between devices  158 us (29%)
  blocking collectives  96.2 us (18%)
  matrix products  42.4 us (8%)
  other arithmetic  32.4 us (6%)
  starting transfers between devices  25 us (5%)
  between operations  14.9 us (3%)
    unnamed x48, local copies, waits for them, and re-layouts  77 us
    psum x1, waiting for transfers between devices, shards(): summed = lax.psum(projected, 'tp')  72.6 us
    all_gather x1, waiting for transfers between devices, shards(): every_query = lax.all_gather(queries, 'seq', axis=0, tiled=True)  53.3 us
    all_to_all x1, blocking collectives, shards(): lax.all_to_all(dispatched, 'seq', split_axis=0, concat_axis=0, tiled=True)  50.3 us
    all_gather x1, blocking collectives, shards(): resid_full = lax.all_gather(hidden_in, 'tp', axis=1, tiled=True)  23.3 us
    all_gather x1, blocking collectives, shards(): everyone = lax.all_gather(picked_rows, 'seq', axis=0, tiled=True)  22.6 us
    gather x8, local copies, waits for them, and re-layouts, cache_block(): picked = jnp.take(cache_kv, block_groups, axis=0)  20.7 us
    mul x3, local copies, waits for them, and re-layouts, shards(): shard_scale[..., None]  14.9 us
  transfers between devices with their start and end apart: 7, of which 6 were waited for; matrix products, arithmetic and copies ran while one was open for 7% of the time, Pallas kernels for 0%

commit v1 on v0

v1 whole, which is shorter than its diff:
```python
import jax
import jax.numpy as jnp
from jax import lax
from jax.experimental import pallas as pl
from jax.experimental.pallas import tpu as pltpu
from jax.sharding import PartitionSpec as P

HQ = 64
KVH = 8
HD = 64
LOW = -1e30
FLOOR = -1e29
MESH = pl.DeviceIdType.MESH
BF = jnp.bfloat16
F32 = jnp.float32


def dot(a, b):
    return jnp.dot(a, b, preferred_element_type=F32)


def dot_tn(a, b):
    return lax.dot_general(a, b, (((0,), (0,)), ((), ())), preferred_element_type=F32)


def place():
    me = lax.axis_index("seq")
    core = me % 2
    chip = me // 2
    return me, core, chip // 4, chip % 4, lax.axis_index("tp")


def shifted(y, x, core, d, sign):
    ny = (y + sign * (d // 4) + 4) % 4
    nx = (x + sign * (d % 4) + 4) % 4
    return (ny * 4 + nx) * 2 + core


def remote(src, dst, send, recv, **where):
    return pltpu.make_async_remote_copy(
        src_ref=src, dst_ref=dst, send_sem=send, recv_sem=recv, device_id=where, device_id_type=MESH
    )


def greet(seq_count, tp_count):
    me, tp = lax.axis_index("seq"), lax.axis_index("tp")
    barrier = pltpu.get_barrier_semaphore()

    def over_seq(d, carry):
        pl.semaphore_signal(
            barrier, inc=1, device_id={"seq": (me + d) % seq_count}, device_id_type=MESH
        )
        return carry

    def over_tp(d, carry):
        pl.semaphore_signal(
            barrier, inc=1, device_id={"tp": (tp + d) % tp_count}, device_id_type=MESH
        )
        return carry

    lax.fori_loop(1, seq_count, over_seq, 0)
    lax.fori_loop(1, tp_count, over_tp, 0)
    pl.semaphore_wait(barrier, seq_count + tp_count - 2)


def attention_kernel(
    group_ref, len_ref, sink_ref, slot_ref, alen_ref,
    query_ref, draft_ref, cache_ref, parents_ref, aidx_ref, wout_ref, hidden_ref, gain_ref,
    normed_ref, stream_ref, tail_ref,
    kv, qin, obuf, sbuf, oin, sin, tbuf, tin, att, wout, proj, zsend, zrecv, gsend, gall, full,
    kv_sem, q_send, q_recv, o_send, o_recv, s_send, s_recv, t_sem, w_sem, z_send, z_recv, g_send, g_recv,
):
    me, core, y, x, tp = place()
    chip = y * 4 + x
    greet(32, 8)

    def send_query(d, carry):
        remote(query_ref, qin.at[d], q_send.at[d], q_recv.at[d], seq=shifted(y, x, core, d, 1)).start()
        return carry

    own_half = pltpu.make_async_copy(cache_ref, kv.at[:, core], kv_sem.at[0])
    own_half.start()
    swap = remote(cache_ref, kv.at[:, core], kv_sem.at[1], kv_sem.at[2], seq=chip * 2 + 1 - core)
    swap.start()
    lax.fori_loop(1, 16, send_query, 0)
    load_w = pltpu.make_async_copy(wout_ref, wout, w_sem)
    load_w.start()

    node = lax.broadcasted_iota(jnp.int32, (16, 64), 1)
    row = lax.broadcasted_iota(jnp.int32, (16, 64), 0)
    chosen = jnp.where((node == aidx_ref[...]) & (row < alen_ref[0]), 1.0, 0.0).astype(BF)
    picked = dot(chosen, draft_ref[...]).astype(BF)
    tbuf[...] = picked
    tin[me] = picked

    def send_tail(d, carry):
        remote(tbuf, tin.at[me], t_sem.at[0], t_sem.at[1], seq=(me + d) % 32).start()
        return carry

    lax.fori_loop(1, 32, send_tail, 0)

    query = query_ref[...]
    qin[0] = query
    draft = draft_ref[...]
    zero_q = jnp.zeros((64, 512), BF)
    up_id = lax.broadcasted_iota(jnp.int32, (64, 64), 0)
    node_id = lax.broadcasted_iota(jnp.int32, (64, 64), 1)
    reach = jnp.where((parents_ref[...] == up_id) | (up_id == node_id), 1.0, 0.0)
    for _ in range(6):
        half = reach.astype(BF)
        reach = jnp.minimum(dot(half, half), 1.0)
    allowed = jnp.concatenate([reach] * 8, axis=1) > 0.5
    tree = jnp.where(allowed, dot(draft, jnp.concatenate([query, zero_q], axis=0)), LOW)
    tree_max = jnp.max(tree, axis=0, keepdims=True)
    tree_weight = jnp.where(allowed, jnp.exp(tree - tree_max), 0.0)
    tree_sum = jnp.sum(tree_weight, axis=0, keepdims=True)
    tree_num = dot_tn(draft, tree_weight.astype(BF))[64:]

    own_half.wait()
    swap.wait()
    position = lax.broadcasted_iota(jnp.int32, (1024, 128), 0) + chip * 1024

    def attend(d, carry):
        request = shifted(y, x, core, d, -1)

        @pl.when(d > 0)
        def _():
            remote(query_ref, qin.at[d], q_send.at[d], q_recv.at[d], seq=request).wait_recv()

        group = group_ref[request]
        length = len_ref[group]
        cached = kv[group].reshape(1024, 128)
        bias = jnp.where(position < length, 0.0, LOW)
        bias = jnp.concatenate([bias, bias], axis=1)
        for part in range(2):
            cols = slice(part * 256, part * 256 + 256)
            ask = jnp.concatenate([qin[d, :, cols], jnp.zeros((64, 256), BF)], axis=0)
            score = dot(cached, ask) + bias
            top = jnp.maximum(jnp.max(score, axis=0, keepdims=True), FLOOR)
            weight = jnp.exp(score - top)
            total = jnp.sum(weight, axis=0, keepdims=True)
            value = dot_tn(cached, weight.astype(BF))[64:]
            value = (value / jnp.maximum(total, 1.0)).astype(BF)
            obuf[d, :, cols] = value
            sbuf[d, 0:1, cols] = top
            sbuf[d, 1:2, cols] = total

        @pl.when(d > 0)
        def _():
            remote(obuf.at[d], oin.at[d], o_send.at[d], o_recv.at[d], seq=request).start()
            remote(sbuf.at[d], sin.at[d], s_send.at[d], s_recv.at[d], seq=request).start()

        return carry

    lax.fori_loop(0, 16, attend, 0)
    oin[0] = obuf[0]
    sin[0] = sbuf[0]

    lane = lax.broadcasted_iota(jnp.int32, (1, 512), 1)
    sink = jnp.zeros((1, 512), F32)
    for h in range(8):
        sink = jnp.where(lane // 64 == h, sink_ref[h], sink)

    def land(d, carry):
        other = shifted(y, x, core, d, 1)
        remote(obuf.at[d], oin.at[d], o_send.at[d], o_recv.at[d], seq=other).wait()
        remote(sbuf.at[d], sin.at[d], s_send.at[d], s_recv.at[d], seq=other).wait()
        remote(query_ref, qin.at[d], q_send.at[d], q_recv.at[d], seq=other).wait_send()
        return carry

    lax.fori_loop(1, 16, land, 0)
    ceiling = jnp.maximum(tree_max, sink)
    for d in range(16):
        ceiling = jnp.maximum(ceiling, sin[d, 0:1])
    tree_scale = jnp.exp(tree_max - ceiling)
    below = tree_scale * tree_sum + jnp.exp(sink - ceiling)
    above = tree_scale * tree_num
    for d in range(16):
        scale = sin[d, 1:2] * jnp.exp(sin[d, 0:1] - ceiling)
        below = below + scale
        above = above + scale * oin[d].astype(F32)
    merged = above / below
    for h in range(8):
        att[:, h * 64 : h * 64 + 64] = merged[:, h * 64 : h * 64 + 64].T
    load_w.wait()
    attended = att[...].astype(BF)
    for n in range(0, 2880, 768):
        n_end = min(n + 768, 2880)
        proj[:, n:n_end] = dot(attended, wout[:, n:n_end])

    for j in range(8):
        zsend[j, :, 0:360] = proj[:, 360 * j : 360 * j + 360].astype(BF)

    def send_piece(d, carry):
        to = (tp + d) % 8
        remote(zsend.at[to], zrecv.at[d], z_send.at[d], z_recv.at[d], tp=to).start()
        return carry

    lax.fori_loop(1, 8, send_piece, 0)
    total = hidden_ref[...].astype(F32) + zsend[tp][:, 0:360].astype(F32)
    for d in range(1, 8):
        remote(zsend.at[d], zrecv.at[d], z_send.at[d], z_recv.at[d], tp=(tp + d) % 8).wait()
        total = total + zrecv[d, :, 0:360].astype(F32)
    stream = total.astype(BF)
    stream_ref[...] = stream
    gsend[:, 0:360] = stream
    gall[tp, :, 0:360] = stream

    def send_stream(d, carry):
        to = (tp + d) % 8
        remote(gsend, gall.at[tp], g_send.at[d], g_recv.at[d], tp=to).start()
        return carry

    lax.fori_loop(1, 8, send_stream, 0)

    def land_stream(d, carry):
        remote(gsend, gall.at[(tp - d + 8) % 8], g_send.at[d], g_recv.at[d], tp=(tp + d) % 8).wait()
        return carry

    lax.fori_loop(1, 8, land_stream, 0)
    for j in range(8):
        full[:, 360 * j : 360 * j + 360] = gall[j, :, 0:360].astype(F32)
    rows = full[...]
    scale = lax.rsqrt(jnp.mean(rows * rows, axis=-1, keepdims=True) + 1e-05)
    normed_ref[...] = (rows * scale * gain_ref[...]).astype(BF)

    def drain_tail(ref, sem):
        pltpu.make_async_copy(ref.at[pl.ds(0, 31)], ref.at[pl.ds(0, 31)], sem).wait()

    drain_tail(tin, t_sem.at[0])
    drain_tail(tin, t_sem.at[1])
    kept = jnp.zeros((16, 128), F32)
    for r in range(32):
        kept = kept + jnp.where(slot_ref[r] == me, tin[r].astype(F32), 0.0)
    tail_ref[...] = kept.astype(BF)


def run_attention(group_of, cache_len, sink, tail_slot, accepted_len, query, draft, cache, parents, aidx, w_out, hidden, gain):
    smem = pl.BlockSpec(memory_space=pltpu.SMEM)
    vmem = pl.BlockSpec(memory_space=pltpu.VMEM)
    hbm = pl.BlockSpec(memory_space=pl.ANY)
    dma = pltpu.SemaphoreType.DMA
    return pl.pallas_call(
        attention_kernel,
        out_shape=(
            jax.ShapeDtypeStruct((64, 2880), BF),
            jax.ShapeDtypeStruct((64, 360), BF),
            jax.ShapeDtypeStruct((16, 128), BF),
        ),
        in_specs=[smem] * 5 + [vmem, vmem, hbm, vmem, vmem, hbm, vmem, vmem],
        out_specs=(vmem, vmem, vmem),
        scratch_shapes=[
            pltpu.VMEM((8, 2, 512, 128), BF),
            pltpu.VMEM((16, 64, 512), BF),
            pltpu.VMEM((16, 64, 512), BF),
            pltpu.VMEM((16, 8, 512), F32),
            pltpu.VMEM((16, 64, 512), BF),
            pltpu.VMEM((16, 8, 512), F32),
            pltpu.VMEM((16, 128), BF),
            pltpu.VMEM((32, 16, 128), BF),
            pltpu.VMEM((64, 512), F32),
            pltpu.VMEM((512, 2880), BF),
            pltpu.VMEM((64, 2880), F32),
            pltpu.VMEM((8, 64, 384), BF),
            pltpu.VMEM((8, 64, 384), BF),
            pltpu.VMEM((64, 384), BF),
            pltpu.VMEM((8, 64, 384), BF),
            pltpu.VMEM((64, 2880), F32),
            dma((3,)), dma((16,)), dma((16,)), dma((16,)), dma((16,)), dma((16,)), dma((16,)),
            dma((2,)), dma, dma((8,)), dma((8,)), dma((8,)), dma((8,)),
        ],
        compiler_params=pltpu.CompilerParams(
            collective_id=0, has_side_effects=True, vmem_limit_bytes=48 * 1024 * 1024
        ),
        name="attend",
    )(group_of, cache_len, sink, tail_slot, accepted_len, query, draft, cache, parents, aidx, w_out, hidden, gain)


CHUNKS = ((0, 768), (768, 1536), (1536, 2304), (2304, 2880))


def expert_kernel(
    routes_ref, weight_ref, normed_ref, stream_ref, wgu_ref, wd_ref,
    out_ref,
    wgu, wd, put, mix, acc_g, acc_u, act, comb, zsend, zrecv,
    d0, d1, d2, d3, r0, r1, r2, r3, b0, b1, b2, b3, g0, g1, g2, g3,
    w_sem, d_send, d_recv, b_send, b_recv, z_send, z_recv,
):
    me, core, y, x, tp = place()
    greet(32, 8)
    sent, arrived, back, got = (d0, d1, d2, d3), (r0, r1, r2, r3), (b0, b1, b2, b3), (g0, g1, g2, g3)
    load_gu = pltpu.make_async_copy(wgu_ref, wgu, w_sem.at[0])
    load_gu.start()
    load_d = pltpu.make_async_copy(wd_ref, wd, w_sem.at[1])
    load_d.start()

    expert_id = lax.broadcasted_iota(jnp.int32, (32, 64), 0)
    member = jnp.zeros((32, 64), F32)
    gain = jnp.zeros((32, 64), F32)
    for k in range(4):
        hit = routes_ref[k : k + 1, :] == expert_id
        member = jnp.where(hit, 1.0, member)
        gain = jnp.where(hit, weight_ref[k : k + 1, :], gain)
    earlier = lax.broadcasted_iota(jnp.int32, (64, 64), 0) < lax.broadcasted_iota(jnp.int32, (64, 64), 1)
    rank = dot(member.astype(BF), jnp.where(earlier, 1.0, 0.0).astype(BF))
    slot = lax.broadcasted_iota(jnp.int32, (16, 64), 0).astype(F32)
    for e in range(32):
        here = (slot == rank[e : e + 1, :]) & (member[e : e + 1, :] > 0.5)
        put[e * 16 : e * 16 + 16, :] = jnp.where(here, 1.0, 0.0).astype(BF)
        mix[e * 16 : e * 16 + 16, :] = jnp.where(here, gain[e : e + 1, :], 0.0)

    def spread(src, dst, send, recv):
        def one(d, carry):
            to = (me + d) % 32
            remote(src.at[to], dst.at[me], send, recv, seq=to).start()
            return carry

        lax.fori_loop(1, 32, one, 0)

    def drain(ref, sem):
        pltpu.make_async_copy(ref.at[pl.ds(0, 31)], ref.at[pl.ds(0, 31)], sem).wait()

    for c, (lo, hi) in enumerate(CHUNKS):
        @pl.loop(0, 4)
        def _(b, c=c, lo=lo, hi=hi):
            rows = put[pl.ds(pl.multiple_of(b * 128, 128), 128), :]
            moved = dot(rows, normed_ref[:, lo:hi]).astype(BF)
            sent[c][pl.ds(b * 8, 8)] = moved.reshape(8, 16, hi - lo)

        spread(sent[c], arrived[c], d_send.at[c], d_recv.at[c])
        arrived[c][me] = sent[c][me]

    weight = mix[...].T
    high = weight.astype(BF)
    low = (weight - high.astype(F32)).astype(BF)
    mixing = jnp.concatenate([high, low], axis=0)

    load_gu.wait()
    for c, (lo, hi) in enumerate(CHUNKS):
        drain(arrived[c], d_recv.at[c])

        @pl.loop(0, 2)
        def _(b, c=c, lo=lo, hi=hi):
            rows = arrived[c][pl.ds(b * 16, 16)].reshape(256, hi - lo)
            span = pl.ds(pl.multiple_of(b * 256, 256), 256)
            gate, up = dot(rows, wgu[0, lo:hi, :]), dot(rows, wgu[1, lo:hi, :])
            if c > 0:
                gate, up = gate + acc_g[span, :], up + acc_u[span, :]
            if c < 3:
                acc_g[span, :] = gate
                acc_u[span, :] = up
            else:
                act[span, :] = (gate * jax.nn.sigmoid(1.702 * gate) * (up + 1.0)).astype(BF)

    load_d.wait()
    for c, (lo, hi) in enumerate(CHUNKS):
        @pl.loop(0, 2)
        def _(b, c=c, lo=lo, hi=hi):
            rows = act[pl.ds(pl.multiple_of(b * 256, 256), 256), :]
            down = dot(rows, wd[:, lo:hi]).astype(BF)
            back[c][pl.ds(b * 16, 16)] = down.reshape(16, 16, hi - lo)

        spread(back[c], got[c], b_send.at[c], b_recv.at[c])
        got[c][me] = back[c][me]

    for c, (lo, hi) in enumerate(CHUNKS):
        drain(got[c], b_recv.at[c])
        both = dot(mixing, got[c][...].reshape(512, hi - lo))
        comb[:, lo:hi] = both[0:64] + both[64:128]
        for j in (2 * c, 2 * c + 1):
            zsend[j, :, 0:360] = comb[:, 360 * j : 360 * j + 360].astype(BF)

    def send_piece(d, carry):
        to = (tp + d) % 8
        remote(zsend.at[to], zrecv.at[d], z_send.at[d], z_recv.at[d], tp=to).start()
        return carry

    lax.fori_loop(1, 8, send_piece, 0)
    total = stream_ref[...].astype(F32) + zsend[tp][:, 0:360].astype(F32)
    for d in range(1, 8):
        remote(zsend.at[d], zrecv.at[d], z_send.at[d], z_recv.at[d], tp=(tp + d) % 8).wait()
        total = total + zrecv[d, :, 0:360].astype(F32)
    out_ref[...] = total.astype(BF)
    for c in range(4):
        drain(sent[c], d_send.at[c])
        drain(back[c], b_send.at[c])


def run_experts(routes, weights, normed, stream, w_gate_up, w_down):
    vmem = pl.BlockSpec(memory_space=pltpu.VMEM)
    hbm = pl.BlockSpec(memory_space=pl.ANY)
    dma = pltpu.SemaphoreType.DMA
    blocks = [pltpu.VMEM((32, 16, hi - lo), BF) for lo, hi in CHUNKS]
    return pl.pallas_call(
        expert_kernel,
        out_shape=jax.ShapeDtypeStruct((64, 360), BF),
        in_specs=[vmem] * 4 + [hbm, hbm],
        out_specs=vmem,
        scratch_shapes=[
            pltpu.VMEM((2, 2880, 360), BF),
            pltpu.VMEM((360, 2880), BF),
            pltpu.VMEM((512, 64), BF),
            pltpu.VMEM((512, 64), F32),
            pltpu.VMEM((512, 360), F32),
            pltpu.VMEM((512, 360), F32),
            pltpu.VMEM((512, 360), BF),
            pltpu.VMEM((64, 2880), F32),
            pltpu.VMEM((8, 64, 384), BF),
            pltpu.VMEM((8, 64, 384), BF),
            *blocks, *blocks, *blocks, *blocks,
            dma((2,)), dma((4,)), dma((4,)), dma((4,)), dma((4,)), dma((8,)), dma((8,)),
        ],
        compiler_params=pltpu.CompilerParams(
            collective_id=1, has_side_effects=True, vmem_limit_bytes=56 * 1024 * 1024
        ),
        name="experts",
    )(routes, weights, normed, stream, w_gate_up, w_down)


def shards(
    queries, draft_kv, cache_kv, cache_len, group_of, parents, sink_logit, w_out, hidden_in,
    norm_gain, routes, route_weight, w_gate_up, w_down, accepted_idx, accepted_len, tail_slot,
):
    query = queries.reshape(64, 8, 64).transpose(2, 1, 0).reshape(64, 512) * BF(0.125)
    normed, stream, tail = run_attention(
        group_of, cache_len, sink_logit, tail_slot, accepted_len,
        query, draft_kv.reshape(64, 128), cache_kv.reshape(8, 512, 128), parents,
        accepted_idx.reshape(16, 1), w_out, hidden_in, norm_gain.reshape(1, 2880),
    )
    out = run_experts(
        routes.T, route_weight.T, normed, stream,
        w_gate_up.reshape(2, 2880, 360), w_down.reshape(360, 2880),
    )
    return (out, tail.reshape(1, 16, 1, 128))


def solution(mesh):
    in_specs = (
        P("seq", None, "tp"),
        P("seq", None, "tp", None),
        P(None, "seq", "tp", None),
        P(),
        P(),
        P("seq", None),
        P("tp"),
        P("tp", None),
        P("seq", "tp"),
        P(),
        P("seq", None),
        P("seq", None),
        P("seq", None, None, "tp"),
        P("seq", "tp", None),
        P("seq", None),
        P("seq"),
        P(),
    )
    out_specs = (P("seq", "tp"), P("seq", None, "tp", None))
    return jax.shard_map(shards, mesh=mesh, in_specs=in_specs, out_specs=out_specs, check_vma=False)
```

time: 536 us -> 183 us (0.34)
  Pallas kernels: 0 us -> 164 us
  waiting for transfers between devices: 158 us -> 0 us
  local copies, waits for them, and re-layouts: 164 us -> 16.3 us
  blocking collectives: 96.2 us -> 0 us
  matrix products: 42.4 us -> 0 us
  other arithmetic: 32.4 us -> 0.85 us
  starting transfers between devices: 25 us -> 0 us
  between operations: 14.9 us -> 1.44 us
    pallas_call x0 -> x2, Pallas kernels: none -> 164 us  [the longest x1 94.2 us: run_experts(): pl.pallas_call(expert_kernel, out_shape=jax.ShapeDtypeStruct((64, 360), B...]
    psum x1 -> x0, waiting for transfers between devices: 72.6 us -> none  [shards(): summed = lax.psum(projected, 'tp')]
    unnamed x48 -> x24, local copies, waits for them, and re-layouts: 77 us -> 14.4 us
    all_gather x1 -> x0, waiting for transfers between devices: 53.3 us -> none  [shards(): every_query = lax.all_gather(queries, 'seq', axis=0, tiled=True)]
    all_to_all x1 -> x0, blocking collectives: 50.3 us -> none  [shards(): lax.all_to_all(dispatched, 'seq', split_axis=0, concat_axis=0, tiled=True)]
    all_gather x2 -> x0, blocking collectives: 45.9 us -> none  [the longest x1 23.3 us: shards(): resid_full = lax.all_gather(hidden_in, 'tp', axis=1, tiled=True)]
    dot_general x21 -> x0, matrix products: 42.4 us -> none  [the longest x4 10.8 us: cache_block(): jnp.einsum('rtkqd,rckd->rkqtc', grouped, cache_keys, preferred_element_ty...]
    gather x15 -> x0, local copies, waits for them, and re-layouts: 27.7 us -> none  [the longest x8 20.7 us: cache_block(): picked = jnp.take(cache_kv, block_groups, axis=0)]
  transfers between devices with their start and end apart: 7 -> 0, of which waited for: 6 -> 0; matrix products, arithmetic and copies ran while one was open for 7% -> 0% of each run, Pallas kernels for 0% -> 0%
where the time goes in v1:
time: 183 us; the launch traced here: 182 us
  Pallas kernels  164 us (90%)
  local copies, waits for them, and re-layouts  16.3 us (9%)
    pallas_call x1, Pallas kernels, run_experts(): pl.pallas_call(expert_kernel, out_shape=jax.ShapeDtypeStruct((64, 360), B...  94.2 us
    pallas_call x1, Pallas kernels, run_attention(): pl.pallas_call(attention_kernel, out_shape=(jax.ShapeDtypeStruct((64, 288...  69.6 us
    unnamed x24, local copies, waits for them, and re-layouts  14.4 us

profile of v1, /device:TPU:1, one launch (start us, length us, event | category | flops | bytes accessed | tf_op | source)
XLA Modules:
  0.0 182.4 jit_solution(17959755562213251810)
XLA Ops:
  1.3 0.7 copy.20.aidx_ref
  2.0 0.7 reshape.34.gain_ref
  2.7 0.8 broadcast_multiply_fusion
  3.6 0.1 mul.14
  3.7 0.2 copy.19
  3.9 0.1 mul.16.query_ref
  4.0 0.0 copy-start.2
  4.0 0.0 copy-start.4
  4.0 0.0 copy-start.5
  4.1 0.0 copy-start.6
  4.1 0.0 copy-start.7
  4.1 0.0 copy-start.8
  4.1 0.0 copy-start.9
  4.1 3.4 %copy.21.wout_ref = bf16[512,2880]{1,0:T(8,128)(2,1)S(1)} copy(bf16[512,2880]{0,1:T(8,128)(2,1)} %param.24) | data formatting | bytes 5898240 | tf_op args[7]
  7.5 0.0 copy-done.2
  7.5 0.0 copy-done.4
  7.5 0.0 copy-done.5
  7.5 0.0 copy-done.6
  7.5 0.0 copy-done.7
  7.5 0.0 copy-done.8
  7.5 0.0 copy-done.9
  7.5 0.0 copy-start
  7.6 1.2 copy-done
  8.8 69.6 %attend.1 = (bf16[64,2880]{1,0:T(8,128)(2,1)S(1)}, bf16[64,360]{1,0:T(8,128)(2,1)S(1)}, bf16[16,128]{1,0:T(8,128)(2,1)S(1)}) custom-call(s32[32]{0:T(128)S(1)} %copy-done.5, s32[8]{0:T(128)S(1)} %copy-done.6, f32[8]{0:T(128)S(1)} %copy-done.7, s32[32]{0:T(128)S(1)} %copy-done.8, s32[1]{0:T(128)S(6)} %copy.25.alen_ref, bf16[64,512]{1,0:T(8,128)(2,1)S(1)} %mul.16.query_ref, ...), custom_call_target="tpu_custom_call" | custom-call | tf_op jit(solution)/shard_map/attend/pallas_call | solution.py:243
  78.4 0.0 copy-start.1
  78.4 0.7 copy-done.1
  79.1 0.0 copy-start.3
  79.1 0.6 copy-done.3
  79.7 6.4 %copy.22 = bf16[1,2,2880,360]{3,2,1,0:T(8,128)(2,1)} copy(bf16[1,2,2880,360]{2,3,1,0:T(8,128)(2,1)} %param.29) | data formatting | bytes 8294400 | tf_op args[12]
  86.2 94.2 %experts.1 = bf16[64,360]{1,0:T(8,128)(2,1)} custom-call(s32[4,64]{1,0:T(4,128)} %bitcast.15, f32[4,64]{1,0:T(4,128)} %bitcast.16, bf16[64,2880]{1,0:T(8,128)(2,1)} %copy-done.1, bf16[64,360]{1,0:T(8,128)(2,1)} %copy-done.3, bf16[2,2880,360]{2,1,0:T(8,128)(2,1)} %bitcast.12, bf16[360,2880]{1,0:T(8,128)(2,1)} %bitcast.13), custom_call_target="tpu_custom_call" | custom-call | tf_op jit(solution)/shard_map/experts/pallas_call | solution.py:394
  180.4 1.4 copy.26
  181.8 0.6 copy.27
Async XLA Ops:
  4.0 3.5 %copy-start.2 = (bf16[64,360]{1,0:T(8,128)(2,1)S(1)}, bf16[64,360]{1,0:T(8,128)(2,1)}, u32[]{:S(2)}) copy-start(bf16[64,360]{1,0:T(8,128)(2,1)} %hidden_ref.1) | copy-start | bytes 138244
  4.0 3.5 %copy-start.4 = (bf16[1,64,1,128]{3,1,2,0:T(8,128)(2,1)S(1)}, bf16[1,64,1,128]{3,1,2,0:T(8,128)(2,1)}, u32[]{:S(2)}) copy-start(bf16[1,64,1,128]{3,1,2,0:T(8,128)(2,1)} %param.18) | copy-start | bytes 49156
  4.0 3.5 %copy-start.5 = (s32[32]{0:T(128)S(1)}, s32[32]{0:T(128)}, u32[]{:S(2)}) copy-start(s32[32]{0:T(128)} %group_ref.1) | copy-start | bytes 388
  4.1 3.5 %copy-start.6 = (s32[8]{0:T(128)S(1)}, s32[8]{0:T(128)}, u32[]{:S(2)}) copy-start(s32[8]{0:T(128)} %len_ref.1) | copy-start | bytes 100
  4.1 3.5 %copy-start.7 = (f32[8]{0:T(128)S(1)}, f32[8]{0:T(128)}, u32[]{:S(2)}) copy-start(f32[8]{0:T(128)} %sink_ref.1) | copy-start | bytes 100
  4.1 3.5 %copy-start.8 = (s32[32]{0:T(128)S(1)}, s32[32]{0:T(128)}, u32[]{:S(2)}) copy-start(s32[32]{0:T(128)} %slot_ref.1) | copy-start | bytes 388
  4.1 3.5 %copy-start.9 = (s32[1,64]{1,0:T(1,128)S(1)}, s32[1,64]{1,0:T(1,128)}, u32[]{:S(2)}) copy-start(s32[1,64]{1,0:T(1,128)} %parents_ref.1) | copy-start | bytes 772
  7.5 1.2 copy-start
  78.4 0.7 copy-start.1
  79.1 0.6 copy-start.3

commit v2 on v1

v2 whole, which is shorter than its diff:
```python
import jax
import jax.numpy as jnp
from jax import lax
from jax.experimental import pallas as pl
from jax.experimental.pallas import tpu as pltpu
from jax.sharding import PartitionSpec as P

LOW = -1e30
FLOOR = -1e29
MESH = pl.DeviceIdType.MESH
BF = jnp.bfloat16
F32 = jnp.float32


def dot(a, b):
    return jnp.dot(a, b, preferred_element_type=F32)


def dot_tn(a, b):
    return lax.dot_general(a, b, (((0,), (0,)), ((), ())), preferred_element_type=F32)


def dot_nt(a, b):
    return lax.dot_general(a, b, (((1,), (1,)), ((), ())), preferred_element_type=F32)


def remote(src, dst, send, recv, **where):
    return pltpu.make_async_remote_copy(
        src_ref=src, dst_ref=dst, send_sem=send, recv_sem=recv, device_id=where, device_id_type=MESH
    )


def loop(lo, hi, body):
    def step(i, carry):
        body(i)
        return carry

    lax.fori_loop(lo, hi, step, 0)


def layer_kernel(
    group_ref, len_ref, sink_ref, slot_ref, alen_ref,
    query_ref, draft_ref, cache_ref, parents_ref, aidx_ref, wout_ref, hidden_ref, gain_ref,
    routes_ref, weight_ref, wgu_ref, wd_ref,
    out_ref, tail_ref,
    kv, qraw, qown, qin, obuf, sbuf, oin, sin, tbuf, tin, att, wout,
    hpad, zsend, zrecv, piece, gall, ssend, srecv, nq,
    wgu, wgp, wd, wdp, put, mix, sent, arrived, zout, zin, keep, back, got, comb, fsend, frecv,
    kv_sem, q_send, q_recv, o_send, o_recv, s_send, s_recv, t_sem, w_sem,
    z_send, z_recv, g_send, g_recv, n_send, n_recv,
    d_send, d_recv, f_send, f_recv, p_send, p_recv, b_send, b_recv, e_send, e_recv,
):
    me, tp = lax.axis_index("seq"), lax.axis_index("tp")
    core, chip = me % 2, me // 2
    y, x = chip // 4, chip % 4
    odd = tp % 2
    need = ((tp + 2) // 4) % 2

    def peer(d, sign, flip=1):
        ny = (y + sign * (d // 4) + 4) % 4
        nx = (x + sign * (d % 4) + 4) % 4
        return (ny * 4 + nx) * 2 + (core + flip) % 2

    def same(d, sign):
        return peer(d, sign, 0)

    def away(d, sign):
        return peer(d // 2, sign, d % 2)

    barrier = pltpu.get_barrier_semaphore()

    def hello(d):
        pl.semaphore_signal(barrier, inc=1, device_id={"seq": away(d, 1)}, device_id_type=MESH)

    def hello_tp(d):
        pl.semaphore_signal(barrier, inc=1, device_id={"tp": (tp + d) % 8}, device_id_type=MESH)

    loop(1, 32, hello)
    loop(1, 8, hello_tp)

    own_half = pltpu.make_async_copy(cache_ref, kv.at[:, core], kv_sem.at[0])
    own_half.start()
    loads = [
        pltpu.make_async_copy(src, dst, w_sem.at[i])
        for i, (src, dst) in enumerate(((wout_ref, wout), (wgu_ref, wgu), (wd_ref, wd)))
    ]
    for load in loads:
        load.start()

    asked = query_ref[...].astype(F32) * 0.125
    for h in range(8):
        qraw[:, h * 64 : h * 64 + 64] = asked[:, h * 64 : h * 64 + 64].T
    query = qraw[...].astype(BF)
    qown[...] = query
    qin[0] = query
    node = lax.broadcasted_iota(jnp.int32, (64, 16), 0)
    row = lax.broadcasted_iota(jnp.int32, (64, 16), 1)
    chosen = jnp.where((node == aidx_ref[...]) & (row < alen_ref[0]), 1.0, 0.0).astype(BF)
    picked = dot_tn(chosen, draft_ref[...]).astype(BF)
    tbuf[...] = picked
    tin[me] = picked

    pl.semaphore_wait(barrier, 38)
    swap = remote(cache_ref, kv.at[:, core], kv_sem.at[1], kv_sem.at[2], seq=chip * 2 + 1 - core)
    swap.start()

    def send_query(d):
        remote(qown, qin.at[d], q_send.at[d], q_recv.at[d], seq=same(d, 1)).start()

    loop(1, 16, send_query)

    def send_tail(d):
        remote(tbuf, tin.at[me], t_sem.at[0], t_sem.at[1], seq=away(d, 1)).start()

    loop(1, 32, send_tail)

    draft = draft_ref[...]
    up_id = lax.broadcasted_iota(jnp.int32, (64, 64), 0)
    node_id = lax.broadcasted_iota(jnp.int32, (64, 64), 1)
    reach = jnp.where((parents_ref[...] == up_id) | (up_id == node_id), 1.0, 0.0)
    for _ in range(6):
        half = reach.astype(BF)
        reach = jnp.minimum(dot(half, half), 1.0)
    allowed = jnp.concatenate([reach] * 8, axis=1) > 0.5
    tree = jnp.where(allowed, dot(draft, jnp.concatenate([query, jnp.zeros((64, 512), BF)], axis=0)), LOW)
    tree_max = jnp.max(tree, axis=0, keepdims=True)
    tree_weight = jnp.where(allowed, jnp.exp(tree - tree_max), 0.0)
    tree_sum = jnp.sum(tree_weight, axis=0, keepdims=True)
    tree_num = dot_tn(draft, tree_weight.astype(BF))[64:]

    own_half.wait()
    swap.wait()
    position = lax.broadcasted_iota(jnp.int32, (1024, 128), 0) + chip * 1024

    def attend(d):
        request = same(d, -1)

        @pl.when(d > 0)
        def _():
            remote(qown, qin.at[d], q_send.at[d], q_recv.at[d], seq=request).wait_recv()

        group = group_ref[request]
        length = len_ref[group]
        cached = kv[group].reshape(1024, 128)
        bias = jnp.where(position < length, 0.0, LOW)
        bias = jnp.concatenate([bias, bias], axis=1)
        for part in range(2):
            cols = slice(part * 256, part * 256 + 256)
            ask = jnp.concatenate([qin[d, :, cols], jnp.zeros((64, 256), BF)], axis=0)
            score = dot(cached, ask) + bias
            top = jnp.maximum(jnp.max(score, axis=0, keepdims=True), FLOOR)
            weight = jnp.exp(score - top)
            total = jnp.sum(weight, axis=0, keepdims=True)
            value = dot_tn(cached, weight.astype(BF))[64:]
            obuf[d, :, cols] = (value / jnp.maximum(total, 1.0)).astype(BF)
            sbuf[d, 0:1, cols] = top
            sbuf[d, 1:2, cols] = total

        @pl.when(d > 0)
        def _():
            remote(obuf.at[d], oin.at[d], o_send.at[d], o_recv.at[d], seq=request).start()
            remote(sbuf.at[d], sin.at[d], s_send.at[d], s_recv.at[d], seq=request).start()

    loop(0, 16, attend)
    oin[0] = obuf[0]
    sin[0] = sbuf[0]

    expert_id = lax.broadcasted_iota(jnp.int32, (32, 64), 0)
    member = jnp.zeros((32, 64), F32)
    given = jnp.zeros((32, 64), F32)
    for k in range(4):
        hit = routes_ref[k : k + 1, :] == expert_id
        member = jnp.where(hit, 1.0, member)
        given = jnp.where(hit, weight_ref[k : k + 1, :], given)
    rank = dot(member.astype(BF), jnp.where(up_id < node_id, 1.0, 0.0).astype(BF))
    slot = lax.broadcasted_iota(jnp.int32, (16, 64), 0).astype(F32)
    for e in range(32):
        here = (slot == rank[e : e + 1, :]) & (member[e : e + 1, :] > 0.5)
        put[e * 16 : e * 16 + 16, :] = jnp.where(here, 1.0, 0.0).astype(BF)
        mix[e * 16 : e * 16 + 16, :] = jnp.where(here, given[e : e + 1, :], 0.0)
    for load in loads:
        load.wait()
    blank = jnp.zeros((360, 24), BF)
    for j in range(8):
        span, wide = slice(360 * j, 360 * j + 360), slice(384 * j, 384 * j + 384)
        wgp[0, :, wide] = jnp.concatenate([wgu[0, :, span], blank], axis=1)
        wgp[1, :, wide] = jnp.concatenate([wgu[1, :, span], blank], axis=1)
        wdp[:, wide] = jnp.concatenate([wd[:, span], blank], axis=1)
    zsend[...] = jnp.zeros((8, 64, 384), BF)
    hpad[...] = jnp.zeros((64, 384), F32)
    hpad[:, 0:360] = hidden_ref[...].astype(F32)

    lane = lax.broadcasted_iota(jnp.int32, (1, 512), 1)
    sink = jnp.zeros((1, 512), F32)
    for h in range(8):
        sink = jnp.where(lane // 64 == h, sink_ref[h], sink)

    def land(d):
        other = same(d, 1)
        remote(obuf.at[d], oin.at[d], o_send.at[d], o_recv.at[d], seq=other).wait()
        remote(sbuf.at[d], sin.at[d], s_send.at[d], s_recv.at[d], seq=other).wait()
        remote(qown, qin.at[d], q_send.at[d], q_recv.at[d], seq=other).wait_send()

    loop(1, 16, land)
    ceiling = jnp.maximum(tree_max, sink)
    for d in range(16):
        ceiling = jnp.maximum(ceiling, sin[d, 0:1])
    tree_scale = jnp.exp(tree_max - ceiling)
    below = tree_scale * tree_sum + jnp.exp(sink - ceiling)
    above = tree_scale * tree_num
    for d in range(16):
        scale = sin[d, 1:2] * jnp.exp(sin[d, 0:1] - ceiling)
        below = below + scale
        above = above + scale * oin[d].astype(F32)
    merged = above / below
    for h in range(8):
        att[:, h * 64 : h * 64 + 64] = merged[:, h * 64 : h * 64 + 64].T
    attended = att[...].astype(BF)
    for j in range(8):
        zsend[j, :, 0:360] = dot_nt(attended, wout[360 * j : 360 * j + 360, :]).astype(BF)

    def send_piece(d):
        to = (tp + d) % 8
        remote(zsend.at[to], zrecv.at[d], z_send.at[d], z_recv.at[d], tp=to).start()

    loop(1, 8, send_piece)
    total = hpad[...] + zsend[tp].astype(F32)
    for d in range(1, 8):
        remote(zsend.at[d], zrecv.at[d], z_send.at[d], z_recv.at[d], tp=(tp + d) % 8).wait()
        total = total + zrecv[d].astype(F32)
    stream = total.astype(BF)
    piece[...] = stream
    stream_f = stream.astype(F32)

    for k in range(4):
        to = 2 * k + need

        @pl.when(to != tp)
        def _(k=k, to=to):
            remote(piece, gall.at[tp % 4], g_send.at[k], g_recv.at[tp % 4], tp=to).start()

        @pl.when(to == tp)
        def _():
            gall[tp % 4] = piece[...]

    squares = jnp.sum(stream_f * stream_f, axis=1, keepdims=True)
    square = jnp.broadcast_to(squares, (64, 128))
    spread_rows = jnp.concatenate([square, square], axis=0).T[0:8]
    ssend[...] = spread_rows

    def send_norm(d):
        remote(ssend, srecv.at[d], n_send.at[d], n_recv.at[d], tp=(tp + d) % 8).start()

    loop(1, 8, send_norm)
    summed = spread_rows
    for d in range(1, 8):
        remote(ssend, srecv.at[d], n_send.at[d], n_recv.at[d], tp=(tp + d) % 8).wait()
        summed = summed + srecv[d]
    column = jnp.concatenate([summed] * 16, axis=0).T[0:64, 0:1]
    inverse = lax.rsqrt(column * (1.0 / 2880.0) + 1e-05)

    for k in range(4):
        source = k + 4 * ((k // 2 + odd) % 2)

        @pl.when(source != tp)
        def _(k=k, source=source):
            remote(piece, gall.at[k], g_send.at[k], g_recv.at[k], tp=source).wait_recv()

    mine = (odd, 3 - odd)
    for h in range(2):
        for i in range(2):
            j = 2 * mine[h] + i
            normed = gall[j % 4].astype(F32) * inverse * gain_ref[j]
            nq[h, :, 384 * i : 384 * i + 384] = normed.astype(BF)

    for h in range(2):
        @pl.loop(0, 4)
        def _(b, h=h):
            rows = put[pl.ds(pl.multiple_of(b * 128, 128), 128), :]
            sent[h, pl.ds(b * 8, 8)] = dot(rows, nq[h]).astype(BF).reshape(8, 16, 768)

    def dispatch(d):
        to = away(d, 1)
        for h in range(2):
            remote(sent.at[h, to], arrived.at[mine[h], d], d_send.at[h], d_recv.at[h, d], seq=to).start()

    loop(1, 32, dispatch)
    for h in range(2):
        arrived[mine[h], 0] = sent[h, me]

    partner = (tp + 1 - 2 * odd, (tp + 7 + 2 * odd) % 8)
    other = (1 - odd, 2 + odd)

    def forward(d):
        for h in range(2):
            @pl.when(d > 0)
            def _(h=h):
                remote(
                    sent.at[h, 0], arrived.at[mine[h], d], d_send.at[h], d_recv.at[h, d], seq=away(d, -1)
                ).wait_recv()

            block = arrived.at[mine[h], d]
            remote(block, block, f_send.at[h], f_recv.at[h, d // 8], tp=partner[h]).start()

    def feed(g):
        for h in range(2):
            block = arrived.at[other[h], pl.ds(g * 8, 8)]
            pltpu.make_async_copy(block, block, f_recv.at[h, g]).wait()
        gate = jnp.zeros((128, 360), F32)
        up = jnp.zeros((128, 360), F32)
        for q in range(4):
            rows = arrived[q, pl.ds(g * 8, 8)].reshape(128, 768)
            cols = slice(768 * q, 768 * q + 768)
            gate = gate + dot_nt(rows, wgp[0, :, cols])
            up = up + dot_nt(rows, wgp[1, :, cols])
        act = (gate * jax.nn.sigmoid(1.702 * gate) * (up + 1.0)).astype(BF)
        for h in range(2):
            far = dot(act, wdp[:, pl.ds(pl.multiple_of(768 * other[h], 128), 768)])
            zout[h, g] = far.astype(BF).reshape(8, 16, 768)
            remote(zout.at[h, g], zin.at[h, g], p_send.at[h, g], p_recv.at[h, g], tp=partner[h]).start()
        for h in range(2):
            keep[h, g] = dot(act, wdp[:, pl.ds(pl.multiple_of(768 * mine[h], 128), 768)])

    def give(g):
        for h in range(2):
            remote(zout.at[h, g], zin.at[h, g], p_send.at[h, g], p_recv.at[h, g], tp=partner[h]).wait()
            both = keep[h, g] + zin[h, g].reshape(128, 768).astype(F32)
            back[h, pl.ds(g * 8, 8)] = both.astype(BF).reshape(8, 16, 768)

        def one(i):
            d = g * 8 + i
            for h in range(2):
                @pl.when(d > 0)
                def _(h=h):
                    to = away(d, -1)
                    remote(back.at[h, d], got.at[h, me], b_send.at[h], b_recv.at[h], seq=to).start()

        loop(0, 8, one)

    def stage(i):
        @pl.when(i < 4)
        def _():
            loop(i * 8, i * 8 + 8, forward)

        @pl.when((i > 0) & (i < 5))
        def _():
            feed(i - 1)

        @pl.when(i > 1)
        def _():
            give(i - 2)

    loop(0, 6, stage)
    for h in range(2):
        got[h, me] = back[h, 0]

    weight = mix[...].T
    high = weight.astype(BF)
    low = (weight - high.astype(F32)).astype(BF)
    mixing = jnp.concatenate([high, low], axis=0)

    def drain(ref, sem):
        pltpu.make_async_copy(ref.at[pl.ds(0, 31)], ref.at[pl.ds(0, 31)], sem).wait()

    for h in range(2):
        drain(got.at[h], b_recv.at[h])
        both = dot(mixing, got[h].reshape(512, 768))
        both = both[0:64] + both[64:128]
        for i in range(2):
            k = 2 * h + i
            to = 2 * mine[h] + i
            fsend[k] = both[:, 384 * i : 384 * i + 384].astype(BF)

            @pl.when(to != tp)
            def _(k=k, to=to):
                remote(fsend.at[k], frecv.at[tp // 2], e_send.at[k], e_recv.at[tp // 2], tp=to).start()

            @pl.when(to == tp)
            def _(k=k):
                frecv[tp // 2] = fsend[k]

    total = piece[...].astype(F32)
    for k in range(4):
        source = 2 * k + need

        @pl.when(source != tp)
        def _(k=k, source=source):
            remote(fsend.at[k], frecv.at[k], e_send.at[k], e_recv.at[k], tp=source).wait_recv()

        total = total + frecv[k].astype(F32)
    out_ref[...] = total[:, 0:360].astype(BF)

    drain(tin, t_sem.at[0])
    drain(tin, t_sem.at[1])
    kept = jnp.zeros((16, 128), F32)
    for r in range(32):
        kept = kept + jnp.where(slot_ref[r] == me, tin[r].astype(F32), 0.0)
    tail_ref[...] = kept.astype(BF)

    for k in range(4):
        @pl.when(2 * k + need != tp)
        def _(k=k):
            remote(piece, gall.at[k], g_send.at[k], g_recv.at[k], tp=2 * k + need).wait_send()

        to = 2 * mine[k // 2] + k % 2

        @pl.when(to != tp)
        def _(k=k, to=to):
            remote(fsend.at[k], frecv.at[k], e_send.at[k], e_recv.at[k], tp=to).wait_send()

    for h in range(2):
        drain(sent.at[h], d_send.at[h])
        drain(back.at[h], b_send.at[h])
        pltpu.make_async_copy(sent.at[h], sent.at[h], f_send.at[h]).wait()


def run_layer(*operands):
    smem = pl.BlockSpec(memory_space=pltpu.SMEM)
    vmem = pl.BlockSpec(memory_space=pltpu.VMEM)
    hbm = pl.BlockSpec(memory_space=pl.ANY)
    dma = pltpu.SemaphoreType.DMA
    return pl.pallas_call(
        layer_kernel,
        out_shape=(jax.ShapeDtypeStruct((64, 360), BF), jax.ShapeDtypeStruct((16, 128), BF)),
        in_specs=[smem] * 5 + [vmem, vmem, hbm, vmem, vmem, hbm, vmem, vmem, vmem, vmem, hbm, hbm],
        out_specs=(vmem, vmem),
        scratch_shapes=[
            pltpu.VMEM((8, 2, 512, 128), BF),
            pltpu.VMEM((64, 512), F32),
            pltpu.VMEM((64, 512), BF),
            pltpu.VMEM((16, 64, 512), BF),
            pltpu.VMEM((16, 64, 512), BF),
            pltpu.VMEM((16, 2, 512), F32),
            pltpu.VMEM((16, 64, 512), BF),
            pltpu.VMEM((16, 2, 512), F32),
            pltpu.VMEM((16, 128), BF),
            pltpu.VMEM((32, 16, 128), BF),
            pltpu.VMEM((64, 512), F32),
            pltpu.VMEM((2880, 512), BF),
            pltpu.VMEM((64, 384), F32),
            pltpu.VMEM((8, 64, 384), BF),
            pltpu.VMEM((8, 64, 384), BF),
            pltpu.VMEM((64, 384), BF),
            pltpu.VMEM((4, 64, 384), BF),
            pltpu.VMEM((8, 128), F32),
            pltpu.VMEM((8, 8, 128), F32),
            pltpu.VMEM((2, 64, 768), BF),
            pltpu.VMEM((2, 360, 2880), BF),
            pltpu.VMEM((2, 360, 3072), BF),
            pltpu.VMEM((360, 2880), BF),
            pltpu.VMEM((360, 3072), BF),
            pltpu.VMEM((512, 64), BF),
            pltpu.VMEM((512, 64), F32),
            pltpu.VMEM((2, 32, 16, 768), BF),
            pltpu.VMEM((4, 32, 16, 768), BF),
            pltpu.VMEM((2, 4, 8, 16, 768), BF),
            pltpu.VMEM((2, 4, 8, 16, 768), BF),
            pltpu.VMEM((2, 4, 128, 768), F32),
            pltpu.VMEM((2, 32, 16, 768), BF),
            pltpu.VMEM((2, 32, 16, 768), BF),
            pltpu.VMEM((8, 128), F32),
            pltpu.VMEM((4, 64, 384), BF),
            pltpu.VMEM((4, 64, 384), BF),
            dma((3,)), dma((16,)), dma((16,)), dma((16,)), dma((16,)), dma((16,)), dma((16,)),
            dma((2,)), dma((3,)),
            dma((8,)), dma((8,)), dma((4,)), dma((4,)), dma((8,)), dma((8,)),
            dma((2,)), dma((2, 32)), dma((2,)), dma((2, 4)), dma((2, 4)), dma((2, 4)),
            dma((2,)), dma((2,)), dma((4,)), dma((4,)),
        ],
        compiler_params=pltpu.CompilerParams(
            collective_id=0, has_side_effects=True, vmem_limit_bytes=62 * 1024 * 1024
        ),
        name="layer",
    )(*operands)


def shards(
    queries, draft_kv, cache_kv, cache_len, group_of, parents, sink_logit, w_out, hidden_in,
    norm_gain, routes, route_weight, w_gate_up, w_down, accepted_idx, accepted_len, tail_slot,
):
    gain = jnp.pad(norm_gain.reshape(8, 1, 360), ((0, 0), (0, 0), (0, 24)))
    out, tail = run_layer(
        group_of, cache_len, sink_logit, tail_slot, accepted_len,
        queries.reshape(64, 512), draft_kv.reshape(64, 128), cache_kv.reshape(8, 512, 128), parents,
        accepted_idx, w_out.T, hidden_in, gain, routes.T, route_weight.T,
        w_gate_up.reshape(2, 2880, 360).transpose(0, 2, 1), w_down.reshape(360, 2880),
    )
    return (out, tail.reshape(1, 16, 1, 128))


def solution(mesh):
    in_specs = (
        P("seq", None, "tp"),
        P("seq", None, "tp", None),
        P(None, "seq", "tp", None),
        P(),
        P(),
        P("seq", None),
        P("tp"),
        P("tp", None),
        P("seq", "tp"),
        P(),
        P("seq", None),
        P("seq", None),
        P("seq", None, None, "tp"),
        P("seq", "tp", None),
        P("seq", None),
        P("seq"),
        P(),
    )
    out_specs = (P("seq", "tp"), P("seq", None, "tp", None))
    return jax.shard_map(shards, mesh=mesh, in_specs=in_specs, out_specs=out_specs, check_vma=False)
```

time: 183 us -> 141 us (0.77)
  Pallas kernels: 164 us -> 134 us
  local copies, waits for them, and re-layouts: 16.3 us -> 4.1 us
    pallas_call x2 -> x1, Pallas kernels: 164 us -> 134 us  [run_layer(): pl.pallas_call(layer_kernel, out_shape=(jax.ShapeDtypeStruct((64, 360), B...]
    unnamed x24 -> x2, local copies, waits for them, and re-layouts: 14.4 us -> 2.69 us
where the time goes in v2:
time: 141 us; the launch traced here: 140 us
  Pallas kernels  134 us (95%)
  local copies, waits for them, and re-layouts  4.1 us (3%)
    pallas_call x1, Pallas kernels, run_layer(): pl.pallas_call(layer_kernel, out_shape=(jax.ShapeDtypeStruct((64, 360), B...  134 us

profile of v2, /device:TPU:1, one launch (start us, length us, event | category | flops | bytes accessed | tf_op | source)
XLA Modules:
  0.0 139.6 jit_solution(3219827976249491604)
XLA Ops:
  1.3 0.8 reshape.28
  2.1 0.6 pad.4.gain_ref
  2.7 134.2 %layer.1 = (bf16[64,360]{1,0:T(8,128)(2,1)}, bf16[16,128]{1,0:T(8,128)(2,1)}) custom-call(s32[32]{0:T(128)} %group_ref.1, s32[8]{0:T(128)} %len_ref.1, f32[8]{0:T(128)} %sink_ref.1, s32[32]{0:T(128)} %slot_ref.1, s32[1]{0:T(128)S(6)} %copy.21.alen_ref, bf16[64,512]{1,0:T(8,128)(2,1)} %bitcast.15, bf16[64,128]{1,0:T(8,128)(2,1)} %bitcast.16, ...), custom_call_target="tpu_custom_call" | custom-call | tf_op jit(solution)/shard_map/layer/pallas_call | solution.py:422
  136.9 1.4 %copy.22 = bf16[64,360]{1,0:T(8,128)(2,1)} copy(bf16[64,360]{1,0:T(8,128)(2,1)} %get-tuple-element.8) | data formatting | bytes 92160
  138.3 1.3 copy.23

commit v3 on v2

--- a/solution.py
+++ b/solution.py
@@ -8,6 +8,11 @@
 LOW = -1e30
 FLOOR = -1e29
 MESH = pl.DeviceIdType.MESH
+GROUPS = 8
+SIZE = 32 // GROUPS
+AHEAD = 4
+FEED_LAG = 3
+GIVE_LAG = 6
 BF = jnp.bfloat16
 F32 = jnp.float32
 
@@ -45,38 +50,40 @@
     out_ref, tail_ref,
     kv, qraw, qown, qin, obuf, sbuf, oin, sin, tbuf, tin, att, wout,
     hpad, zsend, zrecv, piece, gall, ssend, srecv, nq,
-    wgu, wgp, wd, wdp, put, mix, sent, arrived, zout, zin, keep, back, got, comb, fsend, frecv,
+    wgu, wgp, wd, wdp, put, mix, sent, arrived, zout, zin, keep, back, got, gains, fsend, frecv,
     kv_sem, q_send, q_recv, o_send, o_recv, s_send, s_recv, t_sem, w_sem,
     z_send, z_recv, g_send, g_recv, n_send, n_recv,
     d_send, d_recv, f_send, f_recv, p_send, p_recv, b_send, b_recv, e_send, e_recv,
 ):
     me, tp = lax.axis_index("seq"), lax.axis_index("tp")
-    core, chip = me % 2, me // 2
-    y, x = chip // 4, chip % 4
-    odd = tp % 2
+    core, chip = lax.rem(me, 2), lax.div(me, 2)
+    y, x = lax.div(chip, 4), lax.rem(chip, 4)
+    odd = lax.rem(tp, 2)
+    row_at = [lax.rem(y + k, 4) * 8 for k in range(4)]
+    col_at = [lax.rem(x + k, 4) * 2 for k in range(4)]
+    core_at = [core, 1 - core]
+
+    def static_away(d):
+        k = d // 2
+        return row_at[k % 4] + col_at[(k % 4 + k // 4) % 4] + core_at[d % 2]
+
     need = ((tp + 2) // 4) % 2
 
-    def peer(d, sign, flip=1):
-        ny = (y + sign * (d // 4) + 4) % 4
-        nx = (x + sign * (d % 4) + 4) % 4
-        return (ny * 4 + nx) * 2 + (core + flip) % 2
+    def peer(k, sign, flip):
+        step = lax.rem(k, 4)
+        ny = lax.rem(y + sign * step + 4, 4)
+        nx = lax.rem(x + sign * (step + lax.div(k, 4)) + 8, 4)
+        return ny * 8 + nx * 2 + core_at[flip]
 
     def same(d, sign):
         return peer(d, sign, 0)
 
-    def away(d, sign):
-        return peer(d // 2, sign, d % 2)
-
     barrier = pltpu.get_barrier_semaphore()
 
-    def hello(d):
-        pl.semaphore_signal(barrier, inc=1, device_id={"seq": away(d, 1)}, device_id_type=MESH)
-
-    def hello_tp(d):
-        pl.semaphore_signal(barrier, inc=1, device_id={"tp": (tp + d) % 8}, device_id_type=MESH)
-
-    loop(1, 32, hello)
-    loop(1, 8, hello_tp)
+    for d in range(1, 32):
+        pl.semaphore_signal(barrier, inc=1, device_id={"seq": static_away(d)}, device_id_type=MESH)
+    for d in range(1, 8):
+        pl.semaphore_signal(barrier, inc=1, device_id={"tp": lax.rem(tp + d, 8)}, device_id_type=MESH)
 
     own_half = pltpu.make_async_copy(cache_ref, kv.at[:, core], kv_sem.at[0])
     own_half.start()
@@ -107,12 +114,10 @@
     def send_query(d):
         remote(qown, qin.at[d], q_send.at[d], q_recv.at[d], seq=same(d, 1)).start()
 
-    loop(1, 16, send_query)
-
-    def send_tail(d):
-        remote(tbuf, tin.at[me], t_sem.at[0], t_sem.at[1], seq=away(d, 1)).start()
-
-    loop(1, 32, send_tail)
+    loop(1, 4, send_query)
+
+    for d in range(1, 32):
+        remote(tbuf, tin.at[me], t_sem.at[0], t_sem.at[1], seq=static_away(d)).start()
 
     draft = draft_ref[...]
     up_id = lax.broadcasted_iota(jnp.int32, (64, 64), 0)
@@ -132,8 +137,19 @@
     swap.wait()
     position = lax.broadcasted_iota(jnp.int32, (1024, 128), 0) + chip * 1024
 
+    def query_left(d):
+        remote(qown, qin.at[d], q_send.at[d], q_recv.at[d], seq=same(d, 1)).wait_send()
+
     def attend(d):
         request = same(d, -1)
+
+        @pl.when(d % 4 == 0)
+        def _():
+            loop(jnp.maximum(d, 1), d + 4, query_left)
+
+            @pl.when(d < 12)
+            def _():
+                loop(d + 4, d + 8, send_query)
 
         @pl.when(d > 0)
         def _():
@@ -144,10 +160,12 @@
         cached = kv[group].reshape(1024, 128)
         bias = jnp.where(position < length, 0.0, LOW)
         bias = jnp.concatenate([bias, bias], axis=1)
-        for part in range(2):
-            cols = slice(part * 256, part * 256 + 256)
-            ask = jnp.concatenate([qin[d, :, cols], jnp.zeros((64, 256), BF)], axis=0)
-            score = dot(cached, ask) + bias
+        halves = (slice(0, 256), slice(256, 512))
+        scores = [
+            dot(cached, jnp.concatenate([qin[d, :, cols], jnp.zeros((64, 256), BF)], axis=0)) + bias
+            for cols in halves
+        ]
+        for cols, score in zip(halves, scores):
             top = jnp.maximum(jnp.max(score, axis=0, keepdims=True), FLOOR)
             weight = jnp.exp(score - top)
             total = jnp.sum(weight, axis=0, keepdims=True)
@@ -189,6 +207,9 @@
     zsend[...] = jnp.zeros((8, 64, 384), BF)
     hpad[...] = jnp.zeros((64, 384), F32)
     hpad[:, 0:360] = hidden_ref[...].astype(F32)
+    gains[...] = jnp.zeros((8, 1, 384), F32)
+    for j in range(8):
+        gains[j, :, 0:360] = gain_ref[360 * j : 360 * j + 360].reshape(1, 360)
 
     lane = lax.broadcasted_iota(jnp.int32, (1, 512), 1)
     sink = jnp.zeros((1, 512), F32)
@@ -199,7 +220,6 @@
         other = same(d, 1)
         remote(obuf.at[d], oin.at[d], o_send.at[d], o_recv.at[d], seq=other).wait()
         remote(sbuf.at[d], sin.at[d], s_send.at[d], s_recv.at[d], seq=other).wait()
-        remote(qown, qin.at[d], q_send.at[d], q_recv.at[d], seq=other).wait_send()
 
     loop(1, 16, land)
     ceiling = jnp.maximum(tree_max, sink)
@@ -270,7 +290,7 @@
     for h in range(2):
         for i in range(2):
             j = 2 * mine[h] + i
-            normed = gall[j % 4].astype(F32) * inverse * gain_ref[j]
+            normed = gall[j % 4].astype(F32) * inverse * gains[j]
             nq[h, :, 384 * i : 384 * i + 384] = normed.astype(BF)
 
     for h in range(2):
@@ -279,44 +299,58 @@
             rows = put[pl.ds(pl.multiple_of(b * 128, 128), 128), :]
             sent[h, pl.ds(b * 8, 8)] = dot(rows, nq[h]).astype(BF).reshape(8, 16, 768)
 
-    def dispatch(d):
-        to = away(d, 1)
+    def dispatch(g, first=0):
+        for i in range(first, SIZE):
+            to = peer(SIZE // 2 * g + i // 2, 1, i % 2)
+            d = SIZE * g + i
+            for h in range(2):
+                remote(
+                    sent.at[h, to], arrived.at[mine[h], d], d_send.at[h, g], d_recv.at[h, d], seq=to
+                ).start()
+
+    def dispatched(g, count):
         for h in range(2):
-            remote(sent.at[h, to], arrived.at[mine[h], d], d_send.at[h], d_recv.at[h, d], seq=to).start()
-
-    loop(1, 32, dispatch)
+            block = sent.at[h, pl.ds(0, count)]
+            pltpu.make_async_copy(block, block, d_send.at[h, g]).wait()
+
+    dispatch(0, 1)
+    for g in range(1, AHEAD):
+        dispatch(g)
     for h in range(2):
         arrived[mine[h], 0] = sent[h, me]
 
-    partner = (tp + 1 - 2 * odd, (tp + 7 + 2 * odd) % 8)
+    partner = (tp + 1 - 2 * odd, lax.rem(tp + 7 + 2 * odd, 8))
     other = (1 - odd, 2 + odd)
 
-    def forward(d):
-        for h in range(2):
-            @pl.when(d > 0)
-            def _(h=h):
-                remote(
-                    sent.at[h, 0], arrived.at[mine[h], d], d_send.at[h], d_recv.at[h, d], seq=away(d, -1)
-                ).wait_recv()
-
-            block = arrived.at[mine[h], d]
-            remote(block, block, f_send.at[h], f_recv.at[h, d // 8], tp=partner[h]).start()
+    def forward(g):
+        for i in range(SIZE):
+            d = SIZE * g + i
+            for h in range(2):
+                @pl.when(d > 0)
+                def _(h=h, d=d):
+                    remote(
+                        sent.at[h, 0], arrived.at[mine[h], d], d_send.at[h, 0], d_recv.at[h, d],
+                        seq=static_away(1),
+                    ).wait_recv()
+
+                block = arrived.at[mine[h], d]
+                remote(block, block, f_send.at[h], f_recv.at[h, g], tp=partner[h]).start()
 
     def feed(g):
         for h in range(2):
-            block = arrived.at[other[h], pl.ds(g * 8, 8)]
+            block = arrived.at[other[h], pl.ds(g * SIZE, SIZE)]
             pltpu.make_async_copy(block, block, f_recv.at[h, g]).wait()
-        gate = jnp.zeros((128, 360), F32)
-        up = jnp.zeros((128, 360), F32)
+        gate = jnp.zeros((16 * SIZE, 360), F32)
+        up = jnp.zeros((16 * SIZE, 360), F32)
         for q in range(4):
-            rows = arrived[q, pl.ds(g * 8, 8)].reshape(128, 768)
+            rows = arrived[q, pl.ds(g * SIZE, SIZE)].reshape(16 * SIZE, 768)
             cols = slice(768 * q, 768 * q + 768)
             gate = gate + dot_nt(rows, wgp[0, :, cols])
             up = up + dot_nt(rows, wgp[1, :, cols])
         act = (gate * jax.nn.sigmoid(1.702 * gate) * (up + 1.0)).astype(BF)
         for h in range(2):
             far = dot(act, wdp[:, pl.ds(pl.multiple_of(768 * other[h], 128), 768)])
-            zout[h, g] = far.astype(BF).reshape(8, 16, 768)
+            zout[h, g] = far.astype(BF).reshape(SIZE, 16, 768)
             remote(zout.at[h, g], zin.at[h, g], p_send.at[h, g], p_recv.at[h, g], tp=partner[h]).start()
         for h in range(2):
             keep[h, g] = dot(act, wdp[:, pl.ds(pl.multiple_of(768 * mine[h], 128), 768)])
@@ -324,33 +358,43 @@
     def give(g):
         for h in range(2):
             remote(zout.at[h, g], zin.at[h, g], p_send.at[h, g], p_recv.at[h, g], tp=partner[h]).wait()
-            both = keep[h, g] + zin[h, g].reshape(128, 768).astype(F32)
-            back[h, pl.ds(g * 8, 8)] = both.astype(BF).reshape(8, 16, 768)
-
-        def one(i):
-            d = g * 8 + i
+            both = keep[h, g] + zin[h, g].reshape(16 * SIZE, 768).astype(F32)
+            back[h, pl.ds(g * SIZE, SIZE)] = both.astype(BF).reshape(SIZE, 16, 768)
+
+        for i in range(SIZE):
+            to = peer(SIZE // 2 * g + i // 2, -1, i % 2)
+            d = SIZE * g + i
             for h in range(2):
                 @pl.when(d > 0)
-                def _(h=h):
-                    to = away(d, -1)
+                def _(h=h, d=d, to=to):
                     remote(back.at[h, d], got.at[h, me], b_send.at[h], b_recv.at[h], seq=to).start()
 
-        loop(0, 8, one)
-
     def stage(i):
-        @pl.when(i < 4)
-        def _():
-            loop(i * 8, i * 8 + 8, forward)
-
-        @pl.when((i > 0) & (i < 5))
-        def _():
-            feed(i - 1)
-
-        @pl.when(i > 1)
-        def _():
-            give(i - 2)
-
-    loop(0, 6, stage)
+        @pl.when(i == 0)
+        def _():
+            dispatched(0, SIZE - 1)
+
+        @pl.when((i > 0) & (i < GROUPS))
+        def _():
+            dispatched(i, SIZE)
+
+        @pl.when(i < GROUPS - AHEAD)
+        def _():
+            dispatch(i + AHEAD)
+
+        @pl.when(i < GROUPS)
+        def _():
+            forward(i)
+
+        @pl.when((i >= FEED_LAG) & (i < GROUPS + FEED_LAG))
+        def _():
+            feed(i - FEED_LAG)
+
+        @pl.when(i >= GIVE_LAG)
+        def _():
+            give(i - GIVE_LAG)
+
+    loop(0, GROUPS + GIVE_LAG, stage)
     for h in range(2):
         got[h, me] = back[h, 0]
 
@@ -409,7 +453,6 @@
             remote(fsend.at[k], frecv.at[k], e_send.at[k], e_recv.at[k], tp=to).wait_send()
 
     for h in range(2):
-        drain(sent.at[h], d_send.at[h])
         drain(back.at[h], b_send.at[h])
         pltpu.make_async_copy(sent.at[h], sent.at[h], f_send.at[h]).wait()
 
@@ -453,18 +496,18 @@
             pltpu.VMEM((512, 64), F32),
             pltpu.VMEM((2, 32, 16, 768), BF),
             pltpu.VMEM((4, 32, 16, 768), BF),
-            pltpu.VMEM((2, 4, 8, 16, 768), BF),
-            pltpu.VMEM((2, 4, 8, 16, 768), BF),
-            pltpu.VMEM((2, 4, 128, 768), F32),
+            pltpu.VMEM((2, GROUPS, SIZE, 16, 768), BF),
+            pltpu.VMEM((2, GROUPS, SIZE, 16, 768), BF),
+            pltpu.VMEM((2, GROUPS, 16 * SIZE, 768), F32),
             pltpu.VMEM((2, 32, 16, 768), BF),
             pltpu.VMEM((2, 32, 16, 768), BF),
-            pltpu.VMEM((8, 128), F32),
+            pltpu.VMEM((8, 1, 384), F32),
             pltpu.VMEM((4, 64, 384), BF),
             pltpu.VMEM((4, 64, 384), BF),
             dma((3,)), dma((16,)), dma((16,)), dma((16,)), dma((16,)), dma((16,)), dma((16,)),
             dma((2,)), dma((3,)),
             dma((8,)), dma((8,)), dma((4,)), dma((4,)), dma((8,)), dma((8,)),
-            dma((2,)), dma((2, 32)), dma((2,)), dma((2, 4)), dma((2, 4)), dma((2, 4)),
+            dma((2, GROUPS)), dma((2, 32)), dma((2,)), dma((2, GROUPS)), dma((2, GROUPS)), dma((2, GROUPS)),
             dma((2,)), dma((2,)), dma((4,)), dma((4,)),
         ],
         compiler_params=pltpu.CompilerParams(
@@ -474,17 +517,33 @@
     )(*operands)
 
 
+def hand_over_kernel(out_ref, tail_ref, out_to, tail_to):
+    out_to[...] = out_ref[...]
+    tail_to[...] = tail_ref[...]
+
+
+def hand_over(out, tail):
+    vmem = pl.BlockSpec(memory_space=pltpu.VMEM)
+    return pl.pallas_call(
+        hand_over_kernel,
+        out_shape=(jax.ShapeDtypeStruct(out.shape, BF), jax.ShapeDtypeStruct(tail.shape, BF)),
+        in_specs=[vmem, vmem],
+        out_specs=(vmem, vmem),
+        name="hand_over",
+    )(out, tail)
+
+
 def shards(
     queries, draft_kv, cache_kv, cache_len, group_of, parents, sink_logit, w_out, hidden_in,
     norm_gain, routes, route_weight, w_gate_up, w_down, accepted_idx, accepted_len, tail_slot,
 ):
-    gain = jnp.pad(norm_gain.reshape(8, 1, 360), ((0, 0), (0, 0), (0, 24)))
     out, tail = run_layer(
         group_of, cache_len, sink_logit, tail_slot, accepted_len,
         queries.reshape(64, 512), draft_kv.reshape(64, 128), cache_kv.reshape(8, 512, 128), parents,
-        accepted_idx, w_out.T, hidden_in, gain, routes.T, route_weight.T,
+        accepted_idx, w_out.T, hidden_in, norm_gain, routes.T, route_weight.T,
         w_gate_up.reshape(2, 2880, 360).transpose(0, 2, 1), w_down.reshape(360, 2880),
     )
+    out, tail = hand_over(out, tail)
     return (out, tail.reshape(1, 16, 1, 128))
 
 

time: 141 us -> 128 us (0.908)
  Pallas kernels: 134 us -> 125 us
  local copies, waits for them, and re-layouts: 4.1 us -> 0 us
    pallas_call x1, Pallas kernels: 134 us -> 123 us  [run_layer(): pl.pallas_call(layer_kernel, out_shape=(jax.ShapeDtypeStruct((64, 360), B...]
    unnamed x2 -> x0, local copies, waits for them, and re-layouts: 2.69 us -> none
    pallas_call x0 -> x1, Pallas kernels: none -> 1.43 us  [hand_over(): pl.pallas_call(hand_over_kernel, out_shape=(jax.ShapeDtypeStruct(out.shap...]
where the time goes in v3:
time: 128 us; the launch traced here: 126 us
  Pallas kernels  125 us (98%)
  between operations  1.29 us (1%)
    pallas_call x1, Pallas kernels, run_layer(): pl.pallas_call(layer_kernel, out_shape=(jax.ShapeDtypeStruct((64, 360), B...  123 us

profile of v3, /device:TPU:1, one launch (start us, length us, event | category | flops | bytes accessed | tf_op | source)
XLA Modules:
  0.0 126.1 jit_solution(5295065755368707497)
XLA Ops:
  1.3 123.4 %layer.1 = (bf16[64,360]{1,0:T(8,128)(2,1)}, bf16[16,128]{1,0:T(8,128)(2,1)}) custom-call(s32[32]{0:T(128)} %group_ref.1, s32[8]{0:T(128)} %len_ref.1, f32[8]{0:T(128)} %sink_ref.1, s32[32]{0:T(128)} %slot_ref.1, s32[1]{0:T(128)S(6)} %copy.19.alen_ref, bf16[64,512]{1,0:T(8,128)(2,1)} %bitcast.15, bf16[64,128]{1,0:T(8,128)(2,1)} %bitcast.16, ...), custom_call_target="tpu_custom_call" | custom-call | tf_op jit(solution)/shard_map/layer/pallas_call | solution.py:465
  124.7 1.4 %hand_over.1 = (bf16[64,360]{1,0:T(8,128)(2,1)}, bf16[16,128]{1,0:T(8,128)(2,1)}) custom-call(bf16[64,360]{1,0:T(8,128)(2,1)} %get-tuple-element.6.out_ref, bf16[16,128]{1,0:T(8,128)(2,1)} %get-tuple-element.7.tail_ref), custom_call_target="tpu_custom_call" | custom-call | tf_op jit(solution)/shard_map/hand_over/pallas_call | solution.py:527

commit v4 on v3

--- a/solution.py
+++ b/solution.py
@@ -51,7 +51,7 @@
     kv, qraw, qown, qin, obuf, sbuf, oin, sin, tbuf, tin, att, wout,
     hpad, zsend, zrecv, piece, gall, ssend, srecv, nq,
     wgu, wgp, wd, wdp, put, mix, sent, arrived, zout, zin, keep, back, got, gains, fsend, frecv,
-    kv_sem, q_send, q_recv, o_send, o_recv, s_send, s_recv, t_sem, w_sem,
+    kv_sem, q_send, q_recv, h_send, h_recv, o_send, o_recv, s_send, s_recv, t_sem, w_sem,
     z_send, z_recv, g_send, g_recv, n_send, n_recv,
     d_send, d_recv, f_send, f_recv, p_send, p_recv, b_send, b_recv, e_send, e_recv,
 ):
@@ -75,8 +75,13 @@
         nx = lax.rem(x + sign * (step + lax.div(k, 4)) + 8, 4)
         return ny * 8 + nx * 2 + core_at[flip]
 
-    def same(d, sign):
-        return peer(d, sign, 0)
+    def same(n, sign):
+        corner = n - 7
+        dy = jnp.where(n < 4, 0, jnp.where(n < 7, n - 3, 1 + lax.div(jnp.maximum(corner, 0), 3)))
+        dx = jnp.where(n < 4, n, jnp.where(n < 7, 0, 1 + lax.rem(jnp.maximum(corner, 0), 3)))
+        ny = lax.rem(y + sign * dy + 4, 4)
+        nx = lax.rem(x + sign * dx + 4, 4)
+        return ny * 8 + nx * 2 + core
 
     barrier = pltpu.get_barrier_semaphore()
 
@@ -111,11 +116,24 @@
     swap = remote(cache_ref, kv.at[:, core], kv_sem.at[1], kv_sem.at[2], seq=chip * 2 + 1 - core)
     swap.start()
 
-    def send_query(d):
-        remote(qown, qin.at[d], q_send.at[d], q_recv.at[d], seq=same(d, 1)).start()
-
-    loop(1, 4, send_query)
-
+    def along(k):
+        return row_at[0] + col_at[k] + core if k < 4 else row_at[k - 3] + col_at[0] + core
+
+    def first_query(k):
+        return remote(qown, qin.at[k], q_send.at[k], q_recv.at[k], seq=along(k))
+
+    def relayed(axis, a, b):
+        dy, dx = (b, a) if axis == 0 else (a, b)
+        held, slot = (dx, 7 + 3 * (dy - 1) + dx - 1) if axis == 0 else (3 + dy, 7 + 3 * (dy - 1) + dx - 1)
+        half = pl.ds(32 * axis, 32)
+        return remote(
+            qin.at[held, half], qin.at[slot, half], h_send.at[axis, slot], h_recv.at[axis, slot],
+            seq=along(3 + b) if axis == 0 else along(b),
+        )
+
+    for k in range(1, 4):
+        first_query(k).start()
+        first_query(3 + k).start()
     for d in range(1, 32):
         remote(tbuf, tin.at[me], t_sem.at[0], t_sem.at[1], seq=static_away(d)).start()
 
@@ -132,56 +150,6 @@
     tree_weight = jnp.where(allowed, jnp.exp(tree - tree_max), 0.0)
     tree_sum = jnp.sum(tree_weight, axis=0, keepdims=True)
     tree_num = dot_tn(draft, tree_weight.astype(BF))[64:]
-
-    own_half.wait()
-    swap.wait()
-    position = lax.broadcasted_iota(jnp.int32, (1024, 128), 0) + chip * 1024
-
-    def query_left(d):
-        remote(qown, qin.at[d], q_send.at[d], q_recv.at[d], seq=same(d, 1)).wait_send()
-
-    def attend(d):
-        request = same(d, -1)
-
-        @pl.when(d % 4 == 0)
-        def _():
-            loop(jnp.maximum(d, 1), d + 4, query_left)
-
-            @pl.when(d < 12)
-            def _():
-                loop(d + 4, d + 8, send_query)
-
-        @pl.when(d > 0)
-        def _():
-            remote(qown, qin.at[d], q_send.at[d], q_recv.at[d], seq=request).wait_recv()
-
-        group = group_ref[request]
-        length = len_ref[group]
-        cached = kv[group].reshape(1024, 128)
-        bias = jnp.where(position < length, 0.0, LOW)
-        bias = jnp.concatenate([bias, bias], axis=1)
-        halves = (slice(0, 256), slice(256, 512))
-        scores = [
-            dot(cached, jnp.concatenate([qin[d, :, cols], jnp.zeros((64, 256), BF)], axis=0)) + bias
-            for cols in halves
-        ]
-        for cols, score in zip(halves, scores):
-            top = jnp.maximum(jnp.max(score, axis=0, keepdims=True), FLOOR)
-            weight = jnp.exp(score - top)
-            total = jnp.sum(weight, axis=0, keepdims=True)
-            value = dot_tn(cached, weight.astype(BF))[64:]
-            obuf[d, :, cols] = (value / jnp.maximum(total, 1.0)).astype(BF)
-            sbuf[d, 0:1, cols] = top
-            sbuf[d, 1:2, cols] = total
-
-        @pl.when(d > 0)
-        def _():
-            remote(obuf.at[d], oin.at[d], o_send.at[d], o_recv.at[d], seq=request).start()
-            remote(sbuf.at[d], sin.at[d], s_send.at[d], s_recv.at[d], seq=request).start()
-
-    loop(0, 16, attend)
-    oin[0] = obuf[0]
-    sin[0] = sbuf[0]
 
     expert_id = lax.broadcasted_iota(jnp.int32, (32, 64), 0)
     member = jnp.zeros((32, 64), F32)
@@ -211,6 +179,57 @@
     for j in range(8):
         gains[j, :, 0:360] = gain_ref[360 * j : 360 * j + 360].reshape(1, 360)
 
+    own_half.wait()
+    swap.wait()
+    position = lax.broadcasted_iota(jnp.int32, (1024, 128), 0) + chip * 1024
+
+    def attend(d):
+        request = same(d, -1)
+
+        @pl.when(d == 1)
+        def _():
+            for a in range(1, 4):
+                for axis in range(2):
+                    first_query(a + 3 * axis).wait_recv()
+                    for b in range(1, 4):
+                        relayed(axis, a, b).start()
+
+        @pl.when(d > 6)
+        def _():
+            for axis in range(2):
+                half = pl.ds(32 * axis, 32)
+                remote(
+                    qown.at[half], qin.at[d, half], h_send.at[axis, 0], h_recv.at[axis, d], seq=request
+                ).wait_recv()
+
+        group = group_ref[request]
+        length = len_ref[group]
+        cached = kv[group].reshape(1024, 128)
+        bias = jnp.where(position < length, 0.0, LOW)
+        bias = jnp.concatenate([bias, bias], axis=1)
+        halves = (slice(0, 256), slice(256, 512))
+        scores = [
+            dot(cached, jnp.concatenate([qin[d, :, cols], jnp.zeros((64, 256), BF)], axis=0)) + bias
+            for cols in halves
+        ]
+        for cols, score in zip(halves, scores):
+            top = jnp.maximum(jnp.max(score, axis=0, keepdims=True), FLOOR)
+            weight = jnp.exp(score - top)
+            total = jnp.sum(weight, axis=0, keepdims=True)
+            value = dot_tn(cached, weight.astype(BF))[64:]
+            obuf[d, :, cols] = (value / jnp.maximum(total, 1.0)).astype(BF)
+            sbuf[d, 0:1, cols] = top
+            sbuf[d, 1:2, cols] = total
+
+        @pl.when(d > 0)
+        def _():
+            remote(obuf.at[d], oin.at[d], o_send.at[d], o_recv.at[d], seq=request).start()
+            remote(sbuf.at[d], sin.at[d], s_send.at[d], s_recv.at[d], seq=request).start()
+
+    loop(0, 16, attend)
+    oin[0] = obuf[0]
+    sin[0] = sbuf[0]
+
     lane = lax.broadcasted_iota(jnp.int32, (1, 512), 1)
     sink = jnp.zeros((1, 512), F32)
     for h in range(8):
@@ -222,6 +241,11 @@
         remote(sbuf.at[d], sin.at[d], s_send.at[d], s_recv.at[d], seq=other).wait()
 
     loop(1, 16, land)
+    for a in range(1, 4):
+        for axis in range(2):
+            first_query(a + 3 * axis).wait_send()
+            for b in range(1, 4):
+                relayed(axis, a, b).wait_send()
     ceiling = jnp.maximum(tree_max, sink)
     for d in range(16):
         ceiling = jnp.maximum(ceiling, sin[d, 0:1])
@@ -504,7 +528,7 @@
             pltpu.VMEM((8, 1, 384), F32),
             pltpu.VMEM((4, 64, 384), BF),
             pltpu.VMEM((4, 64, 384), BF),
-            dma((3,)), dma((16,)), dma((16,)), dma((16,)), dma((16,)), dma((16,)), dma((16,)),
+            dma((3,)), dma((7,)), dma((7,)), dma((2, 16)), dma((2, 16)), dma((16,)), dma((16,)), dma((16,)), dma((16,)),
             dma((2,)), dma((3,)),
             dma((8,)), dma((8,)), dma((4,)), dma((4,)), dma((8,)), dma((8,)),
             dma((2, GROUPS)), dma((2, 32)), dma((2,)), dma((2, GROUPS)), dma((2, GROUPS)), dma((2, GROUPS)),

time: 128 us -> 123 us (0.961)
  Pallas kernels: 125 us -> 120 us
    pallas_call x1, Pallas kernels: 123 us -> 119 us  [run_layer(): pl.pallas_call(layer_kernel, out_shape=(jax.ShapeDtypeStruct((64, 360), B...]
where the time goes in v4:
time: 123 us; the launch traced here: 122 us
  Pallas kernels  120 us (98%)
  between operations  1.29 us (1%)
    pallas_call x1, Pallas kernels, run_layer(): pl.pallas_call(layer_kernel, out_shape=(jax.ShapeDtypeStruct((64, 360), B...  119 us

profile of v4, /device:TPU:1, one launch (start us, length us, event | category | flops | bytes accessed | tf_op | source)
XLA Modules:
  0.0 121.6 jit_solution(11687384163513458584)
XLA Ops:
  1.3 118.9 %layer.1 = (bf16[64,360]{1,0:T(8,128)(2,1)}, bf16[16,128]{1,0:T(8,128)(2,1)}) custom-call(s32[32]{0:T(128)} %group_ref.1, s32[8]{0:T(128)} %len_ref.1, f32[8]{0:T(128)} %sink_ref.1, s32[32]{0:T(128)} %slot_ref.1, s32[1]{0:T(128)S(6)} %copy.19.alen_ref, bf16[64,512]{1,0:T(8,128)(2,1)} %bitcast.15, bf16[64,128]{1,0:T(8,128)(2,1)} %bitcast.16, ...), custom_call_target="tpu_custom_call" | custom-call | tf_op jit(solution)/shard_map/layer/pallas_call | solution.py:489
  120.2 1.4 %hand_over.1 = (bf16[64,360]{1,0:T(8,128)(2,1)}, bf16[16,128]{1,0:T(8,128)(2,1)}) custom-call(bf16[64,360]{1,0:T(8,128)(2,1)} %get-tuple-element.6.out_ref, bf16[16,128]{1,0:T(8,128)(2,1)} %get-tuple-element.7.tail_ref), custom_call_target="tpu_custom_call" | custom-call | tf_op jit(solution)/shard_map/hand_over/pallas_call | solution.py:551

commit v5 on v4

--- a/solution.py
+++ b/solution.py
@@ -240,22 +240,27 @@
         remote(obuf.at[d], oin.at[d], o_send.at[d], o_recv.at[d], seq=other).wait()
         remote(sbuf.at[d], sin.at[d], s_send.at[d], s_recv.at[d], seq=other).wait()
 
-    loop(1, 16, land)
+    ceiling = jnp.maximum(tree_max, sink)
+    tree_scale = jnp.exp(tree_max - ceiling)
+    below = tree_scale * tree_sum + jnp.exp(sink - ceiling)
+    above = tree_scale * tree_num
+    for first in range(0, 16, 4):
+        loop(max(first, 1), first + 4, land)
+        before = ceiling
+        for d in range(first, first + 4):
+            ceiling = jnp.maximum(ceiling, sin[d, 0:1])
+        fade = jnp.exp(before - ceiling)
+        below = below * fade
+        above = above * fade
+        for d in range(first, first + 4):
+            scale = sin[d, 1:2] * jnp.exp(sin[d, 0:1] - ceiling)
+            below = below + scale
+            above = above + scale * oin[d].astype(F32)
     for a in range(1, 4):
         for axis in range(2):
             first_query(a + 3 * axis).wait_send()
             for b in range(1, 4):
                 relayed(axis, a, b).wait_send()
-    ceiling = jnp.maximum(tree_max, sink)
-    for d in range(16):
-        ceiling = jnp.maximum(ceiling, sin[d, 0:1])
-    tree_scale = jnp.exp(tree_max - ceiling)
-    below = tree_scale * tree_sum + jnp.exp(sink - ceiling)
-    above = tree_scale * tree_num
-    for d in range(16):
-        scale = sin[d, 1:2] * jnp.exp(sin[d, 0:1] - ceiling)
-        below = below + scale
-        above = above + scale * oin[d].astype(F32)
     merged = above / below
     for h in range(8):
         att[:, h * 64 : h * 64 + 64] = merged[:, h * 64 : h * 64 + 64].T

time: 123 us -> 123 us (level)
  no operation moved by 1% of the time
where the time goes in v5:
time: 123 us; the launch traced here: 122 us
  Pallas kernels  120 us (98%)
  between operations  1.29 us (1%)
    pallas_call x1, Pallas kernels, run_layer(): pl.pallas_call(layer_kernel, out_shape=(jax.ShapeDtypeStruct((64, 360), B...  119 us

profile of v5, /device:TPU:1, one launch (start us, length us, event | category | flops | bytes accessed | tf_op | source)
XLA Modules:
  0.0 121.5 jit_solution(2849474100221874229)
XLA Ops:
  1.3 118.8 %layer.1 = (bf16[64,360]{1,0:T(8,128)(2,1)}, bf16[16,128]{1,0:T(8,128)(2,1)}) custom-call(s32[32]{0:T(128)} %group_ref.1, s32[8]{0:T(128)} %len_ref.1, f32[8]{0:T(128)} %sink_ref.1, s32[32]{0:T(128)} %slot_ref.1, s32[1]{0:T(128)S(6)} %copy.19.alen_ref, bf16[64,512]{1,0:T(8,128)(2,1)} %bitcast.15, bf16[64,128]{1,0:T(8,128)(2,1)} %bitcast.16, ...), custom_call_target="tpu_custom_call" | custom-call | tf_op jit(solution)/shard_map/layer/pallas_call | solution.py:494
  120.1 1.4 %hand_over.1 = (bf16[64,360]{1,0:T(8,128)(2,1)}, bf16[16,128]{1,0:T(8,128)(2,1)}) custom-call(bf16[64,360]{1,0:T(8,128)(2,1)} %get-tuple-element.6.out_ref, bf16[16,128]{1,0:T(8,128)(2,1)} %get-tuple-element.7.tail_ref), custom_call_target="tpu_custom_call" | custom-call | tf_op jit(solution)/shard_map/hand_over/pallas_call | solution.py:556

commit v6 on v5

--- a/solution.py
+++ b/solution.py
@@ -273,6 +273,15 @@
         remote(zsend.at[to], zrecv.at[d], z_send.at[d], z_recv.at[d], tp=to).start()
 
     loop(1, 8, send_piece)
+    def drain(ref, sem):
+        pltpu.make_async_copy(ref.at[pl.ds(0, 31)], ref.at[pl.ds(0, 31)], sem).wait()
+
+    drain(tin, t_sem.at[0])
+    drain(tin, t_sem.at[1])
+    kept = jnp.zeros((16, 128), F32)
+    for r in range(32):
+        kept = kept + jnp.where(slot_ref[r] == me, tin[r].astype(F32), 0.0)
+    tail_ref[...] = kept.astype(BF)
     total = hpad[...] + zsend[tp].astype(F32)
     for d in range(1, 8):
         remote(zsend.at[d], zrecv.at[d], z_send.at[d], z_recv.at[d], tp=(tp + d) % 8).wait()
@@ -432,9 +441,6 @@
     low = (weight - high.astype(F32)).astype(BF)
     mixing = jnp.concatenate([high, low], axis=0)
 
-    def drain(ref, sem):
-        pltpu.make_async_copy(ref.at[pl.ds(0, 31)], ref.at[pl.ds(0, 31)], sem).wait()
-
     for h in range(2):
         drain(got.at[h], b_recv.at[h])
         both = dot(mixing, got[h].reshape(512, 768))
@@ -463,12 +469,6 @@
         total = total + frecv[k].astype(F32)
     out_ref[...] = total[:, 0:360].astype(BF)
 
-    drain(tin, t_sem.at[0])
-    drain(tin, t_sem.at[1])
-    kept = jnp.zeros((16, 128), F32)
-    for r in range(32):
-        kept = kept + jnp.where(slot_ref[r] == me, tin[r].astype(F32), 0.0)
-    tail_ref[...] = kept.astype(BF)
 
     for k in range(4):
         @pl.when(2 * k + need != tp)

time: 123 us -> 123 us (level)
  no operation moved by 1% of the time
where the time goes in v6:
time: 123 us; the launch traced here: 122 us
  Pallas kernels  120 us (98%)
  between operations  1.29 us (1%)
    pallas_call x1, Pallas kernels, run_layer(): pl.pallas_call(layer_kernel, out_shape=(jax.ShapeDtypeStruct((64, 360), B...  119 us

profile of v6, /device:TPU:1, one launch (start us, length us, event | category | flops | bytes accessed | tf_op | source)
XLA Modules:
  0.0 121.5 jit_solution(9096841234224555197)
XLA Ops:
  1.3 118.8 %layer.1 = (bf16[64,360]{1,0:T(8,128)(2,1)}, bf16[16,128]{1,0:T(8,128)(2,1)}) custom-call(s32[32]{0:T(128)} %group_ref.1, s32[8]{0:T(128)} %len_ref.1, f32[8]{0:T(128)} %sink_ref.1, s32[32]{0:T(128)} %slot_ref.1, s32[1]{0:T(128)S(6)} %copy.19.alen_ref, bf16[64,512]{1,0:T(8,128)(2,1)} %bitcast.15, bf16[64,128]{1,0:T(8,128)(2,1)} %bitcast.16, ...), custom_call_target="tpu_custom_call" | custom-call | tf_op jit(solution)/shard_map/layer/pallas_call | solution.py:494
  120.1 1.4 %hand_over.1 = (bf16[64,360]{1,0:T(8,128)(2,1)}, bf16[16,128]{1,0:T(8,128)(2,1)}) custom-call(bf16[64,360]{1,0:T(8,128)(2,1)} %get-tuple-element.6.out_ref, bf16[16,128]{1,0:T(8,128)(2,1)} %get-tuple-element.7.tail_ref), custom_call_target="tpu_custom_call" | custom-call | tf_op jit(solution)/shard_map/hand_over/pallas_call | solution.py:556
